TPU v7x, 256 devices: a whole 4x4x8 slice. The times are simulated.
256 devices in a mesh: scen: 16 (over z, core), inst: 16 (over x, y).
Axes of the slice: x: 4, y: 4, z: 8, core: 2. Of those that a mesh axis runs over, the one named last changes fastest.
Arguments:
- shocks: bfloat16 [8192, 2048], P('scen', 'inst'), may hold values from -6 to 6
- loadings: bfloat16 [2048, 65536], P(None, 'inst'), may hold values from -0.125 to 0.125
- delta: float32 [65536], P('inst'), may hold values from -6 to 6
- gamma: float32 [65536], P('inst'), may hold values from -3 to 3
- kappa: float32 [65536], P('inst'), may hold values from -1.2 to 1.2
- book_of: int32 [65536], P('inst'), may hold values from 0 to 255
- bracket_low: int32 [256], replicated, may hold values from -48 to -25
- bracket_high: int32 [256], replicated, may hold values from -24 to 8
- rank: int32 [256], replicated, may hold values from 64 to 128
Outputs:
- contribution: float32 [256, 65536], P('scen', 'inst')
- quantile: float32 [256], P('inst')
Inputs may be any that keep to these rules, and one draw needn't show every extreme that they name: `book_of`: each instrument's book.
All inputs are finite; a program needn't handle non-finite values.
Results may differ from a plain program's by a relative error of at most 0.002.
Values may be sent and summed in bfloat16 or wider, within the bound.
A program may use at most 128 MiB of HBM per device.

v0:
```python
import jax
import jax.numpy as jnp
from jax import lax
from jax.sharding import PartitionSpec as P

PIVOTS = 64
ROUNDS = 3


tail_width = 0.5
bracket_unit = 0.125


def in_order(tiles, dim):
    lengths = list(tiles.shape[1:])
    lengths[dim] *= tiles.shape[0]
    return jnp.moveaxis(tiles, 0, dim).reshape(lengths)


def sent_to_all(shard, axis):
    length = lax.axis_size(axis)
    return lax.all_to_all(
        jnp.broadcast_to(shard[None], (length, *shard.shape)), axis, 0, 0, tiled=True
    )


def collect(shard, axis, dim):
    return in_order(sent_to_all(shard, axis), dim)


def split_up(shard, dim, length):
    before, after = (shard.shape[:dim], shard.shape[dim + 1 :])
    return jnp.moveaxis(shard.reshape(*before, length, -1, *after), dim, 0)


def sent_and_summed(shard, axis, dim):
    length = lax.axis_size(axis)
    tiles = lax.all_to_all(split_up(shard, dim, length), axis, 0, 0, tiled=True)
    return jnp.sum(tiles, axis=0)


def over_copies(shard, axis):
    everything = sent_to_all(shard, axis)
    return jnp.sum(everything, axis=0)


def revalue(moves, delta, gamma, kappa):
    return (moves * (delta + moves * (gamma + moves * kappa))).astype(jnp.bfloat16)


def count_below(book_pnl, pivots):
    group = min(book_pnl.shape[1], 32)
    blocks = book_pnl.T.reshape(-1, group, book_pnl.shape[0])
    pivot_blocks = pivots.reshape(-1, group, pivots.shape[1])

    def one_block(pair):
        values, marks = pair
        return jnp.sum((values[:, :, None] <= marks[:, None, :]).astype(jnp.int32), axis=1)

    return lax.map(one_block, (blocks, pivot_blocks)).reshape(pivots.shape)


def locate(book_pnl, bracket_low, bracket_high, rank, total):
    lower = bracket_low.astype(jnp.float32) * bracket_unit
    upper = bracket_high.astype(jnp.float32) * bracket_unit
    marks = jnp.arange(PIVOTS, dtype=jnp.int32)
    levels = marks.astype(jnp.float32)
    for sweep_index in range(ROUNDS):
        spacing = (upper - lower) / (PIVOTS - 1)
        pivots = lower[:, None] + levels[None, :] * spacing[:, None]
        counts = total(count_below(book_pnl, pivots))
        below = jnp.sum((counts < rank[:, None]).astype(jnp.int32), axis=1)
        chosen = jnp.clip(below, 1, PIVOTS - 1)
        lower = jnp.sum(jnp.where(marks[None, :] == (chosen - 1)[:, None], pivots, 0.0), axis=1)
        upper = jnp.sum(jnp.where(marks[None, :] == chosen[:, None], pivots, 0.0), axis=1)
    return (lower + upper) * 0.5


def body(shocks, loadings, delta, gamma, kappa, book_of, bracket_low, bracket_high, rank):
    inst_cols = loadings.shape[1]
    book_count = bracket_low.shape[0]
    inst_devices = lax.axis_size("inst")
    scale = (book_count / (inst_cols * inst_devices)) ** 0.5
    moves = jnp.dot(collect(shocks, "inst", 1), loadings, preferred_element_type=jnp.float32)
    profit = revalue(moves, delta, gamma, kappa)
    books = jnp.arange(book_count, dtype=jnp.int32)
    onehot = (book_of[:, None] == books[None, :]).astype(jnp.bfloat16)
    partial_sums = jnp.dot(profit, onehot, preferred_element_type=jnp.float32) * scale
    share = book_count // inst_devices
    share_start = lax.axis_index("inst") * share
    own_low = lax.dynamic_slice_in_dim(bracket_low, share_start, share, 0)
    own_high = lax.dynamic_slice_in_dim(bracket_high, share_start, share, 0)
    own_rank = lax.dynamic_slice_in_dim(rank, share_start, share, 0)
    own_pnl = sent_and_summed(partial_sums, "inst", 1)
    every_pnl = lax.all_gather(own_pnl, "scen", axis=0, tiled=True)
    quantile = locate(every_pnl, own_low, own_high, own_rank, lambda counts: counts)
    own_weights = jax.nn.sigmoid((quantile[None, :] - own_pnl) / tail_width).astype(jnp.bfloat16)
    weights = collect(own_weights, "inst", 1)
    mass = over_copies(jnp.sum(weights.astype(jnp.float32), axis=0), "scen")
    rows_here = book_count // lax.axis_size("scen")
    summed = lax.psum_scatter(
        lax.dot_general(
            weights, profit, (((0,), (0,)), ((), ())), preferred_element_type=jnp.float32
        ),
        "scen",
        scatter_dimension=0,
        tiled=True,
    )
    own_mass = lax.dynamic_slice_in_dim(mass, lax.axis_index("scen") * rows_here, rows_here, 0)
    contribution = summed / own_mass[:, None]
    return (contribution, quantile)


def solution(mesh):
    placed = (
        P("scen", "inst"),
        P(None, "inst"),
        P("inst"),
        P("inst"),
        P("inst"),
        P("inst"),
        P(),
        P(),
        P(),
    )
    return jax.shard_map(
        body, mesh=mesh, in_specs=placed, out_specs=(P("scen", "inst"), P("inst")), check_vma=False
    )
```

profile of v0, /device:TPU:8, one launch (start us, length us, event | category | flops | bytes accessed | tf_op | source)
XLA Modules:
  0.0 193.3 jit_solution(15514047174021639084)
XLA Ops:
  7.2 1.0 copy.14
  8.2 0.2 broadcast_in_dim.34
  8.4 33.8 %all_to_all.21 = bf16[16,512,128]{1,2,0:T(8,128)(2,1)S(1)} all-to-all(bf16[16,512,128]{1,2,0:T(8,128)(2,1)S(1)} %broadcast_in_dim.34), channel_id=1, replica_groups=mesh['scen'=16,'inst'=16] {'inst'}, dimensions={0} | all-to-all | bytes 4194304 | tf_op jit(solution)/shard_map/all_to_all | solution.py:22
  42.2 11.7 %fusion.4 = f32[512,4096]{1,0:T(8,128)S(1)} fusion(bf16[512,2048]{0,1:T(8,128)(2,1)S(1)} %bitcast.17, bf16[2048,4096]{1,0:T(8,128)(2,1)} %param.10), kind=kOutput, calls=%fused_computation.42 | convolution fusion | flops 8589934592 | bytes 27262976 | tf_op jit(solution)/shard_map/dot_general | solution.py:84
  54.0 3.7 %fusion.2 = f32[512,256]{0,1:T(8,128)} fusion(s32[4096]{0:T(1024)S(1)} %copy-done.3, f32[512,4096]{1,0:T(8,128)S(1)} %fusion.4, f32[4096]{0:T(1024)S(1)} %copy-done.4, f32[4096]{0:T(1024)S(1)} %copy-done.5, f32[4096]{0:T(1024)S(1)} %copy-done.6), kind=kOutput, calls=%fused_computation.7 | convolution fusion | flops 1087504384 | bytes 8978432 | tf_op jit(solution)/shard_map/dot_general | solution.py:88
  57.7 5.5 %all-to-all-start.1 = ((f32[16,512,16]{1,2,0:T(8,128)}), f32[16,512,16]{1,2,0:T(8,128)S(1)}, u32[]{:S(2)}, u32[]{:S(2)}) async-start(f32[16,512,16]{1,2,0:T(8,128)} %bitcast.3), calls=%async_computation.1 | async-start | bytes 1048576 | tf_op jit(solution)/shard_map/all_to_all | solution.py:38
  63.2 0.1 dynamic_slice.28
  63.3 0.1 convert_multiply_fusion
  63.4 0.1 multiply_add_fusion.2
  63.5 8.7 %all-to-all-done.1 = f32[16,512,16]{1,2,0:T(8,128)S(1)} async-done(((f32[16,512,16]{1,2,0:T(8,128)}), f32[16,512,16]{1,2,0:T(8,128)S(1)}, u32[]{:S(2)}, u32[]{:S(2)}) %all-to-all-start.1) | async-done | bytes 524320 | tf_op jit(solution)/shard_map/all_to_all | solution.py:38
  72.2 21.6 %all_gather.3 = f32[8192,16]{0,1:T(8,128)S(1)} all-gather(f32[512,16]{0,1:T(8,128)S(1)} %reduce_sum.138), channel_id=1, replica_groups=mesh['scen'=16,'inst'=16] {'scen'}, dimensions={0}, use_global_device_ids=true | all-gather | bytes 557056 | tf_op jit(solution)/shard_map/all_gather | solution.py:95
  93.8 3.5 %convert_reduce_fusion.2 = s32[16,64]{1,0:T(8,128)S(1)} fusion(f32[16,64]{1,0:T(8,128)S(1)} %multiply_add_fusion.2, f32[16,8192]{1,0:T(8,128)S(1)} %bitcast.14), kind=kLoop, calls=%fused_computation.2 | loop fusion | flops 25164800 | bytes 532480 | tf_op jit(solution)/shard_map/while/body/eval_jaxpr/reduce_sum | solution.py:58
  97.3 0.2 convert_reduce_fusion.6
  97.5 0.2 select_reduce_fusion.5
  97.8 3.5 %convert_reduce_fusion.1 = s32[16,64]{1,0:T(8,128)S(1)} fusion(f32[16,64]{1,0:T(8,128)S(1)} %multiply_add_fusion.1, f32[16,8192]{1,0:T(8,128)S(1)} %bitcast.15), kind=kLoop, calls=%fused_computation.1 | loop fusion | flops 25164800 | bytes 532480 | tf_op jit(solution)/shard_map/while/body/eval_jaxpr/reduce_sum | solution.py:58
  101.3 0.2 convert_reduce_fusion.5
  101.5 0.2 select_reduce_fusion.3
  101.7 0.1 multiply_add_fusion
  101.8 3.5 %convert_reduce_fusion = s32[16,64]{1,0:T(8,128)S(1)} fusion(f32[16,64]{1,0:T(8,128)S(1)} %multiply_add_fusion, f32[16,8192]{1,0:T(8,128)S(1)} %bitcast.16), kind=kLoop, calls=%fused_computation | loop fusion | flops 25164800 | bytes 532480 | tf_op jit(solution)/shard_map/while/body/eval_jaxpr/reduce_sum | solution.py:58
  105.3 0.2 convert_reduce_fusion.4
  105.5 0.2 select_reduce_fusion
  105.8 0.1 divide_convert_fusion
  105.9 12.1 %all_to_all.22 = bf16[16,512,16]{1,2,0:T(8,128)(2,1)S(1)} all-to-all(bf16[16,512,16]{1,2,0:T(8,128)(2,1)S(1)} %broadcast_in_dim.36), channel_id=1, replica_groups=mesh['scen'=16,'inst'=16] {'inst'}, dimensions={0} | all-to-all | bytes 524288 | tf_op jit(solution)/shard_map/all_to_all | solution.py:22
  118.0 7.4 %fusion.3 = f32[256,4096]{1,0:T(8,128)} fusion(bf16[512,256]{0,1:T(8,128)(2,1)S(1)} %bitcast.18, f32[512,4096]{1,0:T(8,128)} %copy-done.8, f32[4096]{0:T(1024)S(1)} %copy-done.4, f32[4096]{0:T(1024)S(1)} %copy-done.5, f32[4096]{0:T(1024)S(1)} %copy-done.6), kind=kOutput, calls=%fused_computation.41 | convolution fusion | flops 1086324736 | bytes 12894208 | tf_op jit(solution)/shard_map/dot_general | solution.py:102
  125.4 0.1 convert_reduce_fusion.3
  125.6 0.1 broadcast_in_dim.37
  125.6 0.6 broadcast_in_dim.38
  126.3 3.7 %all-to-all-start.3 = ((f32[16,1,256]{2,1,0:T(1,128)}), f32[16,1,256]{2,1,0:T(1,128)S(1)}, u32[]{:S(2)}, u32[]{:S(2)}) async-start(f32[16,1,256]{2,1,0:T(1,128)} %broadcast_in_dim.38), calls=%async_computation.4 | async-start | bytes 32768 | tf_op jit(solution)/shard_map/all_to_all | solution.py:22
  130.0 7.6 %all-to-all-done.3 = f32[16,1,256]{2,1,0:T(1,128)S(1)} async-done(((f32[16,1,256]{2,1,0:T(1,128)}), f32[16,1,256]{2,1,0:T(1,128)S(1)}, u32[]{:S(2)}, u32[]{:S(2)}) %all-to-all-start.3) | async-done | bytes 16416 | tf_op jit(solution)/shard_map/all_to_all | solution.py:22
  137.7 0.1 dynamic_slice.29
  137.7 47.0 %reduce-scatter.2.cloned.1.call-done = f32[16,4096]{1,0:T(8,128)} async-done(((f32[256,4096]{1,0:T(8,128)}), f32[16,4096]{1,0:T(8,128)}) %reduce-scatter.2.cloned.1.call-update) | async-done | bytes 262160 | tf_op jit(solution)/shard_map/reduce_scatter | solution.py:101
  184.7 1.7 broadcast_divide_fusion
  (31 shorter events, 0.3 us)
Async XLA Ops:
  42.2 11.7 %copy-start.3 = (s32[4096]{0:T(1024)S(1)}, s32[4096]{0:T(1024)}, u32[]{:S(2)}) copy-start(s32[4096]{0:T(1024)} %param.14) | copy-start | bytes 49156
  42.2 11.7 %copy-start.4 = (f32[4096]{0:T(1024)S(1)}, f32[4096]{0:T(1024)}, u32[]{:S(2)}) copy-start(f32[4096]{0:T(1024)} %param.13) | copy-start | bytes 49156
  42.2 11.7 %copy-start.5 = (f32[4096]{0:T(1024)S(1)}, f32[4096]{0:T(1024)}, u32[]{:S(2)}) copy-start(f32[4096]{0:T(1024)} %param.12) | copy-start | bytes 49156
  42.2 11.7 %copy-start.6 = (f32[4096]{0:T(1024)S(1)}, f32[4096]{0:T(1024)}, u32[]{:S(2)}) copy-start(f32[4096]{0:T(1024)} %param.11) | copy-start | bytes 49156
  53.9 3.8 %copy-start.8 = (f32[512,4096]{1,0:T(8,128)}, f32[512,4096]{1,0:T(8,128)S(1)}, u32[]{:S(2)}) copy-start(f32[512,4096]{1,0:T(8,128)S(1)} %fusion.4) | copy-start | bytes 25165828
  53.9 9.3 %copy-start.7 = (s32[256]{0:T(256)S(1)}, s32[256]{0:T(256)}, u32[]{:S(2)}) copy-start(s32[256]{0:T(256)} %param.17) | copy-start | bytes 3076
  53.9 9.4 %copy-start.1 = (s32[256]{0:T(256)S(1)}, s32[256]{0:T(256)}, u32[]{:S(2)}) copy-start(s32[256]{0:T(256)} %param.15) | copy-start | bytes 3076
  54.0 9.3 %copy-start.2 = (s32[256]{0:T(256)S(1)}, s32[256]{0:T(256)}, u32[]{:S(2)}) copy-start(s32[256]{0:T(256)} %param.16) | copy-start | bytes 3076
  57.7 14.5 %all-to-all-start.1 = ((f32[16,512,16]{1,2,0:T(8,128)}), f32[16,512,16]{1,2,0:T(8,128)S(1)}, u32[]{:S(2)}, u32[]{:S(2)}) async-start(f32[16,512,16]{1,2,0:T(8,128)} %bitcast.3), calls=%async_computation.1 | async-start | bytes 1048576 | tf_op jit(solution)/shard_map/all_to_all | solution.py:38
  63.2 121.6 %reduce-scatter.2.cloned.1.call-start = ((), (), s32[]{:S(2)}) async-start(), calls=%async_computation.5 | async-start | bytes 4456448 | tf_op jit(solution)/shard_map/reduce_scatter | solution.py:101
  105.7 19.7 %copy-start = (f32[16]{0:T(128)}, f32[16]{0:T(128)S(1)}, u32[]{:S(2)}) copy-start(f32[16]{0:T(128)S(1)} %add_multiply_fusion) | copy-start | bytes 196
  126.3 11.4 %all-to-all-start.3 = ((f32[16,1,256]{2,1,0:T(1,128)}), f32[16,1,256]{2,1,0:T(1,128)S(1)}, u32[]{:S(2)}, u32[]{:S(2)}) async-start(f32[16,1,256]{2,1,0:T(1,128)} %broadcast_in_dim.38), calls=%async_computation.4 | async-start | bytes 32768 | tf_op jit(solution)/shard_map/all_to_all | solution.py:22
Sparse Core Ops, SparseCore 0:
  125.6 59.1 reduce-scatter.1
where the time goes:
time: 194 us; the launch traced here: 193 us
  blocking collectives  67.5 us (35%)
  waiting for transfers between devices  63.3 us (33%)
  matrix products  22.8 us (12%)
  between operations  14.2 us (7%)
  other arithmetic  14.1 us (7%)
  starting transfers between devices  9.23 us (5%)
  local copies, waits for them, and re-layouts  2.12 us (1%)
    reduce_scatter x1, waiting for transfers between devices, body(): lax.psum_scatter(lax.dot_general(weights, profit, (((0,), (0,)), ((), ())...  47 us
    all_to_all x2, blocking collectives, sent_to_all(): lax.all_to_all(jnp.broadcast_to(shard[None], (length, *shard.shape)), axi...  45.9 us
    all_gather x1, blocking collectives, body(): every_pnl = lax.all_gather(own_pnl, 'scen', axis=0, tiled=True)  21.6 us
    dot_general x1, matrix products, body(): jnp.dot(collect(shocks, 'inst', 1), loadings, preferred_element_type=jnp....  11.7 us
    reduce_sum x3, other arithmetic, one_block(): jnp.sum((values[:, :, None] <= marks[:, None, :]).astype(jnp.int32), axis=1)  10.6 us
    all_to_all x1, waiting for transfers between devices, sent_and_summed(): tiles = lax.all_to_all(split_up(shard, dim, length), axis, 0, 0, tiled=True)  8.69 us
    all_to_all x1, waiting for transfers between devices, sent_to_all(): lax.all_to_all(jnp.broadcast_to(shard[None], (length, *shard.shape)), axi...  7.63 us
    dot_general x1, matrix products, body(): lax.dot_general(weights, profit, (((0,), (0,)), ((), ())), preferred_elem...  7.44 us
  transfers between devices with their start and end apart: 3, of which 3 were waited for; matrix products, arithmetic and copies ran while one was open for 1% of the time, Pallas kernels for 0%

commit v1 on v0

v1 whole, which is shorter than its diff:
```python
import functools

import jax
import jax.numpy as jnp
from jax import lax
from jax.experimental import pallas as pl
from jax.experimental.pallas import tpu as pltpu
from jax.sharding import PartitionSpec as P

MESH = pl.DeviceIdType.MESH
F32 = jnp.float32
BF16 = jnp.bfloat16

PIVOTS = 64
ROUNDS = 3
BOOKS = 256
SIDE = 4
N_INST = 16
N_SCEN = 16
RING = 8
SHARE = 16
SCEN_DEV = 512
HALF = 256
FACT_DEV = 128
FACTORS = 2048
INST_DEV = 4096
TILE = 512
TILES = INST_DEV // TILE
CHUNKS = 4
CHUNK = INST_DEV // CHUNKS
SCALE = (BOOKS / (INST_DEV * N_INST)) ** 0.5


def sigmoid(v):
    return 1.0 / (1.0 + jnp.exp(-v))


def kernel(
    shocks, loadings, delta, gamma, kappa, book_of, low, high, rank,
    out, qout,
    LH, LD, PR, OH, SENS, BK, PS, RS, ROWS, DV, PNL, QR, QA, W,
    SIBS, SIBR, OWNC, RSND, RRCV, OUT,
    ld_sem, in_sem, a_send, a_recv, c_send, c_recv, d_send, d_recv, g_send, g_recv,
    f_send, f_recv, sib_send, sib_recv, r_send, r_recv, o_sem,
):
    s = lax.axis_index("scen")
    i = lax.axis_index("inst")
    x, y = lax.div(i, SIDE), lax.rem(i, SIDE)
    z, c = lax.div(s, 2), lax.rem(s, 2)

    def inst_at(dx, dy):
        return lax.rem(x + dx + SIDE, SIDE) * SIDE + lax.rem(y + dy + SIDE, SIDE)

    def inst_peer(k):
        return lax.rem(i + k, N_INST)

    def scen_peer(k):
        return lax.rem(s + k, N_SCEN)

    def ring_pos(d):
        return lax.rem(z + d + RING, RING)

    def remote(src, dst, ssem, rsem, **dev):
        return pltpu.make_async_remote_copy(
            src_ref=src, dst_ref=dst, send_sem=ssem, recv_sem=rsem,
            device_id=dev, device_id_type=MESH,
        )

    def drain(ref, sem):
        pltpu.make_async_copy(ref, ref, sem).wait()

    own_cols = pl.ds(pl.multiple_of(i * FACT_DEV, FACT_DEV), FACT_DEV)
    small = [
        pltpu.make_async_copy(shocks, LH.at[:, own_cols], in_sem.at[0]),
        pltpu.make_async_copy(delta, SENS.at[0], in_sem.at[1]),
        pltpu.make_async_copy(gamma, SENS.at[1], in_sem.at[2]),
        pltpu.make_async_copy(kappa, SENS.at[2], in_sem.at[3]),
        pltpu.make_async_copy(book_of, BK, in_sem.at[4]),
    ]
    for cp in small:
        cp.start()

    def load_tile(n):
        return pltpu.make_async_copy(
            loadings.at[:, pl.ds(pl.multiple_of(n * TILE, TILE), TILE)], LD.at[n], ld_sem.at[n]
        )

    for n in range(TILES):
        load_tile(n).start()

    barrier = pltpu.get_barrier_semaphore()

    def greet(k, carry):
        pl.semaphore_signal(barrier, inc=1, device_id={"inst": inst_peer(k)}, device_id_type=MESH)
        pl.semaphore_signal(barrier, inc=1, device_id={"scen": scen_peer(k)}, device_id_type=MESH)
        return carry

    lax.fori_loop(1, 16, greet, 0)
    pl.semaphore_wait(barrier, 30)

    def along(colour, first, second):
        return inst_at(first, second) if colour == 0 else inst_at(second, first)

    def rows_of(h, colour, part):
        start = h * HALF + colour * (HALF // 2)
        size = HALF // 2
        if part == 1:
            size //= 2
        elif part == 2:
            size //= 2
            start += size
        return pl.ds(start, size)

    def piece(h, colour, a, b, part):
        k = along(colour, a, b)
        return LH.at[rows_of(h, colour, part), pl.ds(pl.multiple_of(k * FACT_DEV, FACT_DEV), FACT_DEV)]

    def a_pass(h, colour, a, b, part, to_first, to_second, pid):
        there = piece(h, colour, a, b, part)
        src = shocks.at[rows_of(h, colour, part), :] if (a, b) == (0, 0) else there
        remote(
            src, there, a_send, a_recv.at[(h * 2 + colour) * 20 + pid],
            inst=along(colour, to_first, to_second),
        ).start()

    def a_wait(h, colour, a, b, part, pid):
        drain(piece(h, colour, a, b, part), a_recv.at[(h * 2 + colour) * 20 + pid])

    lanes = (0, -1, 1, 2)

    def a_second(h, colour, q):
        a_pass(h, colour, lanes[q], 0, 0, 0, 1, 4 + 4 * q)
        a_pass(h, colour, lanes[q], 0, 0, 0, -1, 5 + 4 * q)

    def a_hand_on(h, colour, q):
        a_wait(h, colour, lanes[q], -1, 0, 4 + 4 * q)
        a_pass(h, colour, lanes[q], -1, 1, 0, 1, 6 + 4 * q)
        a_wait(h, colour, lanes[q], 1, 0, 5 + 4 * q)
        a_pass(h, colour, lanes[q], 1, 2, 0, -1, 7 + 4 * q)

    def a_step(h, step):
        for colour in range(2):
            if step == 0:
                a_pass(h, colour, 0, 0, 0, 1, 0, 0)
                a_pass(h, colour, 0, 0, 0, -1, 0, 1)
                a_second(h, colour, 0)
            elif step == 1:
                a_wait(h, colour, -1, 0, 0, 0)
                a_pass(h, colour, -1, 0, 1, 1, 0, 2)
                a_second(h, colour, 1)
                a_wait(h, colour, 1, 0, 0, 1)
                a_pass(h, colour, 1, 0, 2, -1, 0, 3)
                a_second(h, colour, 2)
            elif step == 2:
                a_hand_on(h, colour, 0)
            elif step == 3:
                a_wait(h, colour, 2, 0, 1, 2)
                a_wait(h, colour, 2, 0, 2, 3)
                a_second(h, colour, 3)
            elif step == 4:
                a_hand_on(h, colour, 1)
                a_hand_on(h, colour, 2)
            elif step == 5:
                a_hand_on(h, colour, 3)
            else:
                for q in range(4):
                    a_wait(h, colour, lanes[q], 2, 1, 6 + 4 * q)
                    a_wait(h, colour, lanes[q], 2, 2, 7 + 4 * q)

    a_step(0, 0)
    small[4].wait()
    book_ids = lax.broadcasted_iota(jnp.int32, (BOOKS, TILE), 0)

    def one_hot(n, carry):
        cols = pl.ds(pl.multiple_of(n * TILE, TILE), TILE)
        OH[:, cols] = jnp.where(BK[:, cols] == book_ids, 1.0, 0.0).astype(BF16)
        return carry

    lax.fori_loop(0, TILES, one_hot, 0)
    for step in range(1, 4):
        a_step(0, step)
    a_step(1, 0)
    a_step(0, 4)
    a_step(0, 5)
    for cp in small[:4]:
        cp.wait()
    a_step(0, 6)

    def share_rows(k):
        return pl.ds(pl.multiple_of(k * SHARE, SHARE), SHARE)

    def send_sums(h):
        def one(k, carry):
            p = inst_peer(k)
            remote(PS.at[h, share_rows(p), :], RS.at[h, i], c_send.at[h], c_recv.at[h], inst=p).start()
            return carry

        lax.fori_loop(1, N_INST, one, 0)
        RS[h, i] = PS[h, share_rows(i), :]

    def take_sums(h):
        drain(RS.at[h, pl.ds(0, N_INST - 1)], c_recv.at[h])
        total = RS[h, 0]
        for k in range(1, N_INST):
            total = total + RS[h, k]
        total = total * SCALE
        PNL[i, h] = total
        for r in range(2):
            ROWS[h, :, r, :] = total[:, r * 128 : (r + 1) * 128]

        def one(k, carry):
            p = scen_peer(k)
            remote(ROWS.at[h, p], DV.at[h, s], d_send.at[h], d_recv.at[h], scen=p).start()
            return carry

        lax.fori_loop(1, N_SCEN, one, 0)

        def other(k, carry):
            p = inst_peer(k)
            remote(PNL.at[i, h], PNL.at[i, h], g_send.at[h], g_recv.at[h], inst=p).start()
            return carry

        lax.fori_loop(1, N_INST, other, 0)
        DV[h, s] = ROWS[h, s]

    def tile(h, n):
        cols = pl.ds(pl.multiple_of(n * TILE, TILE), TILE)
        moves = jnp.dot(LH[pl.ds(h * HALF, HALF), :], LD[n], preferred_element_type=F32)
        d, g, k = SENS[0, :, cols], SENS[1, :, cols], SENS[2, :, cols]
        profit = (moves * (d + moves * (g + moves * k))).astype(BF16)
        PR[pl.ds(h * HALF, HALF), cols] = profit
        part = lax.dot_general(OH[:, cols], profit, (((1,), (1,)), ((), ())), preferred_element_type=F32)
        PS[h] += part

    PS[...] = jnp.zeros_like(PS)

    def first_half(n, carry):
        load_tile(n).wait()
        tile(0, n)
        for step in range(1, 6):
            @pl.when(n == step)
            def _():
                a_step(1, step)
        return carry

    lax.fori_loop(0, TILES, first_half, 0)
    send_sums(0)
    a_step(1, 6)

    def second_half(n, carry):
        tile(1, n)

        @pl.when(n == 5)
        def _():
            take_sums(0)

        return carry

    lax.fori_loop(0, TILES, second_half, 0)
    send_sums(1)
    take_sums(1)

    book = i * SHARE + s
    lower = jnp.full((PIVOTS, 128), low[book], jnp.int32).astype(F32) * 0.125
    upper = jnp.full((PIVOTS, 128), high[book], jnp.int32).astype(F32) * 0.125
    wanted = jnp.full((PIVOTS, 128), rank[book], jnp.int32).astype(F32)
    levels = lax.broadcasted_iota(jnp.int32, (PIVOTS, 128), 0).astype(F32)
    for h in range(2):
        drain(DV.at[h, pl.ds(0, N_SCEN - 1)], d_recv.at[h])
    for _ in range(ROUNDS):
        spacing = (upper - lower) / (PIVOTS - 1)
        marks = lower + levels * spacing
        count = jnp.zeros((PIVOTS, 128), F32)
        for h in range(2):
            for p in range(N_SCEN):
                for r in range(2):
                    row = DV[h, p, pl.ds(r, 1), :]
                    count = count + jnp.where(row <= marks, 1.0, 0.0)
        count = jnp.sum(count, axis=1, keepdims=True)
        below = jnp.sum(jnp.where(count < wanted, 1.0, 0.0), axis=0, keepdims=True)
        chosen = jnp.clip(below, 1.0, PIVOTS - 1.0)
        upper = lower + chosen * spacing
        lower = lower + (chosen - 1.0) * spacing
    quantile = (lower + upper) * 0.5
    pair_q = quantile[0:2, :]
    mass = jnp.zeros((2, 128), F32)
    for h in range(2):
        for p in range(N_SCEN):
            mass = mass + sigmoid((pair_q - DV[h, p]) * 2.0).astype(BF16).astype(F32)
    mass = jnp.sum(jnp.sum(mass, axis=1, keepdims=True), axis=0, keepdims=True)
    lane = lax.broadcasted_iota(jnp.int32, (1, 128), 1)
    QR[s] = jnp.where(lane < 64, quantile[0:1, :], jnp.broadcast_to(mass, (1, 128)))

    def send_q(k, carry):
        remote(QR.at[s], QR.at[s], f_send.at[0], f_recv.at[0], scen=scen_peer(k)).start()
        return carry

    lax.fori_loop(1, N_SCEN, send_q, 0)
    drain(QR.at[pl.ds(0, N_SCEN - 1)], f_recv.at[0])

    def send_all_q(k, carry):
        remote(QR, QA.at[i], f_send.at[1], f_recv.at[1], inst=inst_peer(k)).start()
        return carry

    lax.fori_loop(1, N_INST, send_all_q, 0)
    QA[i] = QR[...]
    q_copy = pltpu.make_async_copy(QR, qout, in_sem.at[5])
    q_copy.start()
    for h in range(2):
        drain(PNL.at[pl.ds(0, N_INST - 1), h], g_recv.at[h])
    drain(QA.at[pl.ds(0, N_INST - 1)], f_recv.at[1])

    for t in range(N_INST):
        place = jnp.where(c == t % 2, BOOKS // 2, 0) + (t // 2) * SHARE
        q = QA[t, :, 0, :][:, 0:1]
        for h in range(2):
            w = sigmoid((q - PNL[t, h]) * 2.0).astype(BF16)
            W[pl.ds(pl.multiple_of(place, SHARE), SHARE), pl.ds(h * HALF, HALF)] = w

    own_mass = QA[s, :, 0, :][:, 64:65]

    def sib_copy(n):
        return remote(SIBS.at[n], SIBR.at[n], sib_send.at[n], sib_recv.at[n], scen=z * 2 + (1 - c))

    def contribute(n):
        for u in range(2):
            width = CHUNK // 2
            cols = pl.ds(n * CHUNK + u * width, width)
            both = jnp.dot(W[...], PR[:, cols], preferred_element_type=F32)
            SIBS[n, :, pl.ds(u * width, width)] = both[: BOOKS // 2].astype(BF16)
            OWNC[n, :, pl.ds(u * width, width)] = both[BOOKS // 2 :]
        sib_copy(n).start()

    def ring_copy(n, way, step):
        if step == 0:
            cols = pl.ds(way * (CHUNK // 2), CHUNK // 2)
        else:
            cols = pl.ds(0, CHUNK)
        slot = (n * 2 + way) * 4 + step
        return remote(
            RSND.at[slot, :, cols], RRCV.at[slot, :, cols], r_send.at[slot], r_recv.at[slot],
            scen=ring_pos(1 if way == 0 else -1) * 2 + c,
        )

    def held(n, dest, cols):
        rows = pl.ds(pl.multiple_of(dest * SHARE, SHARE), SHARE)
        return OWNC[n, rows, cols] + SIBR[n, rows, cols].astype(F32)

    def ring_step(n, step):
        halves = (pl.ds(0, CHUNK // 2), pl.ds(CHUNK // 2, CHUNK // 2))
        if step == 4:
            ring_copy(n, 0, 3).wait_recv()
            ring_copy(n, 1, 3).wait_recv()
            total = held(n, z, pl.ds(0, CHUNK))
            total = total + RRCV[(n * 2) * 4 + 3].astype(F32) + RRCV[(n * 2 + 1) * 4 + 3].astype(F32)
            OUT[:, pl.ds(n * CHUNK, CHUNK)] = total / own_mass
            out_copy(n).start()
            return
        for way in range(2):
            slot = (n * 2 + way) * 4 + step
            dest = ring_pos((4 - step) * (1 if way == 0 else -1))
            if step == 0:
                RSND[slot, :, halves[way]] = held(n, dest, halves[way]).astype(BF16)
            else:
                ring_copy(n, way, step - 1).wait_recv()
                for u in range(2):
                    v = held(n, dest, halves[u])
                    if step > 1 or u == way:
                        v = v + RRCV[slot - 1, :, halves[u]].astype(F32)
                    RSND[slot, :, halves[u]] = v.astype(BF16)
            ring_copy(n, way, step).start()

    def out_copy(n):
        cols = pl.ds(n * CHUNK, CHUNK)
        return pltpu.make_async_copy(OUT.at[:, cols], out.at[:, cols], o_sem.at[n])

    for t in range(CHUNKS + 5):
        if t < CHUNKS:
            contribute(t)
        for n in range(CHUNKS):
            step = t - n - 1
            if step == 0:
                sib_copy(n).wait_recv()
            if 0 <= step <= 4:
                ring_step(n, step)

    drain(LH.at[pl.ds(0, SCEN_DEV * 15 // 16), :], a_send)
    for h in range(2):
        drain(RS.at[h, pl.ds(0, N_INST - 1)], c_send.at[h])
        drain(DV.at[h, pl.ds(0, N_SCEN - 1)], d_send.at[h])
        drain(PNL.at[pl.ds(0, N_INST - 1), h], g_send.at[h])
    drain(QR.at[pl.ds(0, N_SCEN - 1)], f_send.at[0])
    drain(QA.at[pl.ds(0, N_INST - 1)], f_send.at[1])
    q_copy.wait()
    for n in range(CHUNKS):
        sib_copy(n).wait_send()
        for way in range(2):
            for step in range(4):
                ring_copy(n, way, step).wait_send()
        out_copy(n).wait()


def body(shocks, loadings, delta, gamma, kappa, book_of, bracket_low, bracket_high, rank):
    anywhere = pl.BlockSpec(memory_space=pl.ANY)
    scalars = pl.BlockSpec(memory_space=pltpu.SMEM)
    row = lambda v: v.reshape(1, INST_DEV)
    dma = pltpu.SemaphoreType.DMA
    out, q = pl.pallas_call(
        kernel,
        out_shape=(
            jax.ShapeDtypeStruct((SHARE, INST_DEV), F32),
            jax.ShapeDtypeStruct((SHARE, 1, 128), F32),
        ),
        in_specs=[anywhere] * 6 + [scalars] * 3,
        out_specs=(anywhere, anywhere),
        scratch_shapes=[
            pltpu.VMEM((SCEN_DEV, FACTORS), BF16),
            pltpu.VMEM((TILES, FACTORS, TILE), BF16),
            pltpu.VMEM((SCEN_DEV, INST_DEV), BF16),
            pltpu.VMEM((BOOKS, INST_DEV), BF16),
            pltpu.VMEM((3, 1, INST_DEV), F32),
            pltpu.VMEM((1, INST_DEV), jnp.int32),
            pltpu.VMEM((2, BOOKS, HALF), F32),
            pltpu.VMEM((2, N_INST, SHARE, HALF), F32),
            pltpu.VMEM((2, SHARE, 2, 128), F32),
            pltpu.VMEM((2, N_SCEN, 2, 128), F32),
            pltpu.VMEM((N_INST, 2, SHARE, HALF), F32),
            pltpu.VMEM((SHARE, 1, 128), F32),
            pltpu.VMEM((N_INST, SHARE, 1, 128), F32),
            pltpu.VMEM((BOOKS, SCEN_DEV), BF16),
            pltpu.VMEM((CHUNKS, BOOKS // 2, CHUNK), BF16),
            pltpu.VMEM((CHUNKS, BOOKS // 2, CHUNK), BF16),
            pltpu.VMEM((CHUNKS, BOOKS // 2, CHUNK), F32),
            pltpu.VMEM((CHUNKS * 8, SHARE, CHUNK), BF16),
            pltpu.VMEM((CHUNKS * 8, SHARE, CHUNK), BF16),
            pltpu.VMEM((SHARE, INST_DEV), F32),
            dma((TILES,)),
            dma((6,)),
            dma(()),
            dma((80,)),
            dma((2,)), dma((2,)),
            dma((2,)), dma((2,)),
            dma((2,)), dma((2,)),
            dma((2,)), dma((2,)),
            dma((CHUNKS,)), dma((CHUNKS,)),
            dma((CHUNKS * 8,)), dma((CHUNKS * 8,)),
            dma((CHUNKS,)),
        ],
        compiler_params=pltpu.CompilerParams(
            collective_id=0, has_side_effects=True, vmem_limit_bytes=60 * 1024 * 1024
        ),
        name="revalue",
    )(
        shocks, loadings, row(delta), row(gamma), row(kappa), row(book_of),
        bracket_low, bracket_high, rank,
    )
    return out, q[:, 0, 0]


def solution(mesh):
    placed = (
        P("scen", "inst"),
        P(None, "inst"),
        P("inst"),
        P("inst"),
        P("inst"),
        P("inst"),
        P(),
        P(),
        P(),
    )
    return jax.shard_map(
        body, mesh=mesh, in_specs=placed, out_specs=(P("scen", "inst"), P("inst")), check_vma=False
    )
```

time: 194 us -> 101 us (0.52)
  Pallas kernels: 0 us -> 96.9 us
  blocking collectives: 67.5 us -> 0 us
  waiting for transfers between devices: 63.3 us -> 0 us
  matrix products: 22.8 us -> 0 us
  other arithmetic: 14.1 us -> 0 us
  between operations: 14.2 us -> 0.64 us
  starting transfers between devices: 9.23 us -> 0 us
    pallas_call x0 -> x1, Pallas kernels: none -> 96.9 us  [body(): pl.pallas_call(kernel, out_shape=(jax.ShapeDtypeStruct((SHARE, INST_DEV),...]
    reduce_scatter x1 -> x0, waiting for transfers between devices: 47 us -> none  [body(): lax.psum_scatter(lax.dot_general(weights, profit, (((0,), (0,)), ((), ())...]
    all_to_all x2 -> x0, blocking collectives: 45.9 us -> none  [sent_to_all(): lax.all_to_all(jnp.broadcast_to(shard[None], (length, *shard.shape)), axi...]
    dot_general x3 -> x0, matrix products: 22.8 us -> none  [the longest x1 11.7 us: body(): jnp.dot(collect(shocks, 'inst', 1), loadings, preferred_element_type=jnp....]
    all_gather x1 -> x0, blocking collectives: 21.6 us -> none  [body(): every_pnl = lax.all_gather(own_pnl, 'scen', axis=0, tiled=True)]
    all_to_all x2 -> x0, waiting for transfers between devices: 16.3 us -> none  [the longest x1 8.69 us: sent_and_summed(): tiles = lax.all_to_all(split_up(shard, dim, length), axis, 0, 0, tiled=True)]
    reduce_sum x12 -> x0, other arithmetic: 11.9 us -> none  [the longest x3 10.6 us: one_block(): jnp.sum((values[:, :, None] <= marks[:, None, :]).astype(jnp.int32), axis=1)]
    all_to_all x2 -> x0, starting transfers between devices: 9.2 us -> none  [the longest x1 5.47 us: sent_and_summed(): tiles = lax.all_to_all(split_up(shard, dim, length), axis, 0, 0, tiled=True)]
  transfers between devices with their start and end apart: 3 -> 0, of which waited for: 3 -> 0; matrix products, arithmetic and copies ran while one was open for 1% -> 0% of each run, Pallas kernels for 0% -> 0%
where the time goes in v1:
time: 101 us
  Pallas kernels  96.9 us (96%)
  local copies, waits for them, and re-layouts  3.08 us (3%)
    pallas_call x1, Pallas kernels, body(): pl.pallas_call(kernel, out_shape=(jax.ShapeDtypeStruct((SHARE, INST_DEV),...  96.9 us

profile of v1, /device:TPU:8, one launch (start us, length us, event | category | flops | bytes accessed | tf_op | source)
XLA Modules:
  0.0 100.6 jit_solution(8451316637038622663)
XLA Ops:
  0.6 96.9 %revalue.1 = (f32[16,4096]{1,0:T(8,128)}, f32[16,1,128]{2,1,0:T(1,128)}) custom-call(bf16[512,128]{1,0:T(8,128)(2,1)} %shocks.1, bf16[2048,4096]{1,0:T(8,128)(2,1)} %loadings.1, f32[1,4096]{1,0:T(1,128)} %bitcast.4, f32[1,4096]{1,0:T(1,128)} %bitcast.5, f32[1,4096]{1,0:T(1,128)} %bitcast.6, s32[1,4096]{1,0:T(1,128)} %bitcast.7, s32[256]{0:T(256)} %low.1, ...), custom_call_target="tpu_custom_call" | custom-call | tf_op jit(solution)/shard_map/revalue/pallas_call | solution.py:408
  97.5 1.4 %slice_reduce_fusion = f32[16]{0:T(128)} fusion(f32[16,1,128]{2,1,0:T(1,128)} %get-tuple-element.5), kind=kLoop, calls=%fused_computation | loop fusion | bytes 128 | tf_op jit(solution)/shard_map/slice | solution.py:457
  98.9 1.7 %copy.12 = f32[16,4096]{1,0:T(8,128)} copy(f32[16,4096]{1,0:T(8,128)} %get-tuple-element.8) | data formatting | bytes 524288

commit v2 on v1

--- a/solution.py
+++ b/solution.py
@@ -28,6 +28,12 @@
 TILES = INST_DEV // TILE
 CHUNKS = 4
 CHUNK = INST_DEV // CHUNKS
+PLACES = (
+    (0, 0), (-1, 0), (1, 0), (0, -1), (0, 1),
+    (-1, -1), (-1, 1), (1, -1), (1, 1), (2, 0), (0, 2),
+    (2, -1), (2, 1), (-1, 2), (1, 2), (2, 2),
+)
+CUTS = (0, 4, 10, 16)
 SCALE = (BOOKS / (INST_DEV * N_INST)) ** 0.5
 
 
@@ -38,10 +44,10 @@
 def kernel(
     shocks, loadings, delta, gamma, kappa, book_of, low, high, rank,
     out, qout,
-    LH, LD, PR, OH, SENS, BK, PS, RS, ROWS, DV, PNL, QR, QA, W,
-    SIBS, SIBR, OWNC, RSND, RRCV, OUT,
+    LH, LD, ACC, PR, OH, SENS, BK, PS, RS, ROWS, DV, PNL, QR, QA, W,
+    SIBS, SIBR, OWNC, RSND, RRCV,
     ld_sem, in_sem, a_send, a_recv, c_send, c_recv, d_send, d_recv, g_send, g_recv,
-    f_send, f_recv, sib_send, sib_recv, r_send, r_recv, o_sem,
+    f_send, f_recv, sib_send, sib_recv, r_send, r_recv,
 ):
     s = lax.axis_index("scen")
     i = lax.axis_index("inst")
@@ -69,9 +75,8 @@
     def drain(ref, sem):
         pltpu.make_async_copy(ref, ref, sem).wait()
 
-    own_cols = pl.ds(pl.multiple_of(i * FACT_DEV, FACT_DEV), FACT_DEV)
     small = [
-        pltpu.make_async_copy(shocks, LH.at[:, own_cols], in_sem.at[0]),
+        pltpu.make_async_copy(shocks, LH.at[:, pl.ds(0, FACT_DEV)], in_sem.at[0]),
         pltpu.make_async_copy(delta, SENS.at[0], in_sem.at[1]),
         pltpu.make_async_copy(gamma, SENS.at[1], in_sem.at[2]),
         pltpu.make_async_copy(kappa, SENS.at[2], in_sem.at[3]),
@@ -80,13 +85,16 @@
     for cp in small:
         cp.start()
 
-    def load_tile(n):
+    def load_block(p):
+        source = inst_at(*PLACES[p])
         return pltpu.make_async_copy(
-            loadings.at[:, pl.ds(pl.multiple_of(n * TILE, TILE), TILE)], LD.at[n], ld_sem.at[n]
+            loadings.at[pl.ds(pl.multiple_of(source * FACT_DEV, FACT_DEV), FACT_DEV), :],
+            LD.at[pl.ds(p * FACT_DEV, FACT_DEV), :],
+            ld_sem.at[p],
         )
 
-    for n in range(TILES):
-        load_tile(n).start()
+    for p in range(N_INST):
+        load_block(p).start()
 
     barrier = pltpu.get_barrier_semaphore()
 
@@ -101,73 +109,79 @@
     def along(colour, first, second):
         return inst_at(first, second) if colour == 0 else inst_at(second, first)
 
-    def rows_of(h, colour, part):
-        start = h * HALF + colour * (HALF // 2)
-        size = HALF // 2
-        if part == 1:
+    def place_of(colour, a, b):
+        fold = lambda v: (v + 1) % SIDE - 1
+        return PLACES.index((fold(a), fold(b)) if colour == 0 else (fold(b), fold(a)))
+
+    def rows_of(colour, part):
+        start, size = colour * HALF, HALF
+        if part:
             size //= 2
-        elif part == 2:
-            size //= 2
-            start += size
+            start += size * (part - 1)
         return pl.ds(start, size)
 
-    def piece(h, colour, a, b, part):
-        k = along(colour, a, b)
-        return LH.at[rows_of(h, colour, part), pl.ds(pl.multiple_of(k * FACT_DEV, FACT_DEV), FACT_DEV)]
-
-    def a_pass(h, colour, a, b, part, to_first, to_second, pid):
-        there = piece(h, colour, a, b, part)
-        src = shocks.at[rows_of(h, colour, part), :] if (a, b) == (0, 0) else there
+    def piece(colour, a, b, part):
+        return LH.at[rows_of(colour, part), pl.ds(place_of(colour, a, b) * FACT_DEV, FACT_DEV)]
+
+    def a_pass(colour, a, b, part, first, second, pid):
+        if (a, b) == (0, 0):
+            src = shocks.at[rows_of(colour, part), :]
+        else:
+            src = piece(colour, a, b, part)
         remote(
-            src, there, a_send, a_recv.at[(h * 2 + colour) * 20 + pid],
-            inst=along(colour, to_first, to_second),
+            src, piece(colour, a - first, b - second, part), a_send, a_recv.at[colour * 20 + pid],
+            inst=along(colour, first, second),
         ).start()
 
-    def a_wait(h, colour, a, b, part, pid):
-        drain(piece(h, colour, a, b, part), a_recv.at[(h * 2 + colour) * 20 + pid])
+    def a_wait(colour, a, b, part, pid):
+        drain(piece(colour, a, b, part), a_recv.at[colour * 20 + pid])
 
     lanes = (0, -1, 1, 2)
 
-    def a_second(h, colour, q):
-        a_pass(h, colour, lanes[q], 0, 0, 0, 1, 4 + 4 * q)
-        a_pass(h, colour, lanes[q], 0, 0, 0, -1, 5 + 4 * q)
-
-    def a_hand_on(h, colour, q):
-        a_wait(h, colour, lanes[q], -1, 0, 4 + 4 * q)
-        a_pass(h, colour, lanes[q], -1, 1, 0, 1, 6 + 4 * q)
-        a_wait(h, colour, lanes[q], 1, 0, 5 + 4 * q)
-        a_pass(h, colour, lanes[q], 1, 2, 0, -1, 7 + 4 * q)
-
-    def a_step(h, step):
+    def a_second(colour, q):
+        a_pass(colour, lanes[q], 0, 0, 0, 1, 4 + 4 * q)
+        a_pass(colour, lanes[q], 0, 0, 0, -1, 5 + 4 * q)
+
+    def a_hand_on(colour, q):
+        a_wait(colour, lanes[q], -1, 0, 4 + 4 * q)
+        a_pass(colour, lanes[q], -1, 1, 0, 1, 6 + 4 * q)
+        a_wait(colour, lanes[q], 1, 0, 5 + 4 * q)
+        a_pass(colour, lanes[q], 1, 2, 0, -1, 7 + 4 * q)
+
+    def a_last(colour, q):
+        a_wait(colour, lanes[q], 2, 1, 6 + 4 * q)
+        a_wait(colour, lanes[q], 2, 2, 7 + 4 * q)
+
+    def a_step(step):
         for colour in range(2):
             if step == 0:
-                a_pass(h, colour, 0, 0, 0, 1, 0, 0)
-                a_pass(h, colour, 0, 0, 0, -1, 0, 1)
-                a_second(h, colour, 0)
+                a_pass(colour, 0, 0, 0, 1, 0, 0)
+                a_pass(colour, 0, 0, 0, -1, 0, 1)
+                a_second(colour, 0)
             elif step == 1:
-                a_wait(h, colour, -1, 0, 0, 0)
-                a_pass(h, colour, -1, 0, 1, 1, 0, 2)
-                a_second(h, colour, 1)
-                a_wait(h, colour, 1, 0, 0, 1)
-                a_pass(h, colour, 1, 0, 2, -1, 0, 3)
-                a_second(h, colour, 2)
+                a_wait(colour, -1, 0, 0, 0)
+                a_pass(colour, -1, 0, 1, 1, 0, 2)
+                a_second(colour, 1)
+                a_wait(colour, 1, 0, 0, 1)
+                a_pass(colour, 1, 0, 2, -1, 0, 3)
+                a_second(colour, 2)
             elif step == 2:
-                a_hand_on(h, colour, 0)
+                a_hand_on(colour, 0)
             elif step == 3:
-                a_wait(h, colour, 2, 0, 1, 2)
-                a_wait(h, colour, 2, 0, 2, 3)
-                a_second(h, colour, 3)
+                a_wait(colour, 2, 0, 1, 2)
+                a_wait(colour, 2, 0, 2, 3)
+                a_second(colour, 3)
             elif step == 4:
-                a_hand_on(h, colour, 1)
-                a_hand_on(h, colour, 2)
+                a_hand_on(colour, 1)
+                a_hand_on(colour, 2)
+                a_last(colour, 0)
             elif step == 5:
-                a_hand_on(h, colour, 3)
+                a_hand_on(colour, 3)
             else:
-                for q in range(4):
-                    a_wait(h, colour, lanes[q], 2, 1, 6 + 4 * q)
-                    a_wait(h, colour, lanes[q], 2, 2, 7 + 4 * q)
-
-    a_step(0, 0)
+                for q in range(1, 4):
+                    a_last(colour, q)
+
+    a_step(0)
     small[4].wait()
     book_ids = lax.broadcasted_iota(jnp.int32, (BOOKS, TILE), 0)
 
@@ -177,14 +191,11 @@
         return carry
 
     lax.fori_loop(0, TILES, one_hot, 0)
-    for step in range(1, 4):
-        a_step(0, step)
-    a_step(1, 0)
-    a_step(0, 4)
-    a_step(0, 5)
+    PS[...] = jnp.zeros_like(PS)
+    a_step(1)
+    a_step(2)
     for cp in small[:4]:
         cp.wait()
-    a_step(0, 6)
 
     def share_rows(k):
         return pl.ds(pl.multiple_of(k * SHARE, SHARE), SHARE)
@@ -223,41 +234,62 @@
         lax.fori_loop(1, N_INST, other, 0)
         DV[h, s] = ROWS[h, s]
 
-    def tile(h, n):
-        cols = pl.ds(pl.multiple_of(n * TILE, TILE), TILE)
-        moves = jnp.dot(LH[pl.ds(h * HALF, HALF), :], LD[n], preferred_element_type=F32)
+    def factors(group):
+        return pl.ds(CUTS[group] * FACT_DEV, (CUTS[group + 1] - CUTS[group]) * FACT_DEV)
+
+    def wait_blocks(group):
+        for p in range(CUTS[group], CUTS[group + 1]):
+            load_block(p).wait()
+
+    def tile_cols(n):
+        return pl.ds(pl.multiple_of(n * TILE, TILE), TILE)
+
+    def first_group(n, carry):
+        cols = tile_cols(n)
+        ACC[:, cols] = jnp.dot(LH[:, factors(0)], LD[factors(0), cols], preferred_element_type=F32)
+        return carry
+
+    def second_group(n, carry):
+        cols = tile_cols(n)
+        ACC[:, cols] += jnp.dot(LH[:, factors(1)], LD[factors(1), cols], preferred_element_type=F32)
+
+        @pl.when(n == 4)
+        def _():
+            a_step(5)
+
+        return carry
+
+    def last_group(h, n):
+        cols = tile_cols(n)
+        rows = pl.ds(h * HALF, HALF)
+        moves = ACC[rows, cols] + jnp.dot(LH[rows, factors(2)], LD[factors(2), cols], preferred_element_type=F32)
         d, g, k = SENS[0, :, cols], SENS[1, :, cols], SENS[2, :, cols]
         profit = (moves * (d + moves * (g + moves * k))).astype(BF16)
-        PR[pl.ds(h * HALF, HALF), cols] = profit
+        PR[rows, cols] = profit
         part = lax.dot_general(OH[:, cols], profit, (((1,), (1,)), ((), ())), preferred_element_type=F32)
         PS[h] += part
 
-    PS[...] = jnp.zeros_like(PS)
-
-    def first_half(n, carry):
-        load_tile(n).wait()
-        tile(0, n)
-        for step in range(1, 6):
-            @pl.when(n == step)
-            def _():
-                a_step(1, step)
-        return carry
-
-    lax.fori_loop(0, TILES, first_half, 0)
+    def last_first(n, carry):
+        last_group(0, n)
+        return carry
+
+    def last_second(n, carry):
+        last_group(1, n)
+        return carry
+
+    wait_blocks(0)
+    lax.fori_loop(0, TILES, first_group, 0)
+    a_step(3)
+    a_step(4)
+    wait_blocks(1)
+    lax.fori_loop(0, TILES, second_group, 0)
+    a_step(6)
+    wait_blocks(2)
+    lax.fori_loop(0, TILES, last_first, 0)
     send_sums(0)
-    a_step(1, 6)
-
-    def second_half(n, carry):
-        tile(1, n)
-
-        @pl.when(n == 5)
-        def _():
-            take_sums(0)
-
-        return carry
-
-    lax.fori_loop(0, TILES, second_half, 0)
+    lax.fori_loop(0, TILES, last_second, 0)
     send_sums(1)
+    take_sums(0)
     take_sums(1)
 
     book = i * SHARE + s
@@ -304,8 +336,7 @@
 
     lax.fori_loop(1, N_INST, send_all_q, 0)
     QA[i] = QR[...]
-    q_copy = pltpu.make_async_copy(QR, qout, in_sem.at[5])
-    q_copy.start()
+    qout[...] = QR[...]
     for h in range(2):
         drain(PNL.at[pl.ds(0, N_INST - 1), h], g_recv.at[h])
     drain(QA.at[pl.ds(0, N_INST - 1)], f_recv.at[1])
@@ -353,8 +384,7 @@
             ring_copy(n, 1, 3).wait_recv()
             total = held(n, z, pl.ds(0, CHUNK))
             total = total + RRCV[(n * 2) * 4 + 3].astype(F32) + RRCV[(n * 2 + 1) * 4 + 3].astype(F32)
-            OUT[:, pl.ds(n * CHUNK, CHUNK)] = total / own_mass
-            out_copy(n).start()
+            out[:, pl.ds(n * CHUNK, CHUNK)] = total / own_mass
             return
         for way in range(2):
             slot = (n * 2 + way) * 4 + step
@@ -370,19 +400,19 @@
                     RSND[slot, :, halves[u]] = v.astype(BF16)
             ring_copy(n, way, step).start()
 
-    def out_copy(n):
-        cols = pl.ds(n * CHUNK, CHUNK)
-        return pltpu.make_async_copy(OUT.at[:, cols], out.at[:, cols], o_sem.at[n])
-
-    for t in range(CHUNKS + 5):
-        if t < CHUNKS:
-            contribute(t)
-        for n in range(CHUNKS):
-            step = t - n - 1
-            if step == 0:
-                sib_copy(n).wait_recv()
-            if 0 <= step <= 4:
-                ring_step(n, step)
+    for n in range(CHUNKS):
+        contribute(n)
+    for n in range(CHUNKS):
+        sib_copy(n).wait_recv()
+        ring_step(n, 0)
+    for n in range(CHUNKS):
+        ring_step(n, 1)
+    for n in range(CHUNKS):
+        ring_step(n, 2)
+    for n in range(CHUNKS):
+        ring_step(n, 3)
+    for n in range(CHUNKS):
+        ring_step(n, 4)
 
     drain(LH.at[pl.ds(0, SCEN_DEV * 15 // 16), :], a_send)
     for h in range(2):
@@ -391,13 +421,11 @@
         drain(PNL.at[pl.ds(0, N_INST - 1), h], g_send.at[h])
     drain(QR.at[pl.ds(0, N_SCEN - 1)], f_send.at[0])
     drain(QA.at[pl.ds(0, N_INST - 1)], f_send.at[1])
-    q_copy.wait()
     for n in range(CHUNKS):
         sib_copy(n).wait_send()
         for way in range(2):
             for step in range(4):
                 ring_copy(n, way, step).wait_send()
-        out_copy(n).wait()
 
 
 def body(shocks, loadings, delta, gamma, kappa, book_of, bracket_low, bracket_high, rank):
@@ -412,10 +440,11 @@
             jax.ShapeDtypeStruct((SHARE, 1, 128), F32),
         ),
         in_specs=[anywhere] * 6 + [scalars] * 3,
-        out_specs=(anywhere, anywhere),
+        out_specs=(pl.BlockSpec(memory_space=pltpu.VMEM),) * 2,
         scratch_shapes=[
             pltpu.VMEM((SCEN_DEV, FACTORS), BF16),
-            pltpu.VMEM((TILES, FACTORS, TILE), BF16),
+            pltpu.VMEM((FACTORS, INST_DEV), BF16),
+            pltpu.VMEM((SCEN_DEV, INST_DEV), F32),
             pltpu.VMEM((SCEN_DEV, INST_DEV), BF16),
             pltpu.VMEM((BOOKS, INST_DEV), BF16),
             pltpu.VMEM((3, 1, INST_DEV), F32),
@@ -433,18 +462,16 @@
             pltpu.VMEM((CHUNKS, BOOKS // 2, CHUNK), F32),
             pltpu.VMEM((CHUNKS * 8, SHARE, CHUNK), BF16),
             pltpu.VMEM((CHUNKS * 8, SHARE, CHUNK), BF16),
-            pltpu.VMEM((SHARE, INST_DEV), F32),
-            dma((TILES,)),
-            dma((6,)),
+            dma((N_INST,)),
+            dma((5,)),
             dma(()),
-            dma((80,)),
+            dma((40,)),
             dma((2,)), dma((2,)),
             dma((2,)), dma((2,)),
             dma((2,)), dma((2,)),
             dma((2,)), dma((2,)),
             dma((CHUNKS,)), dma((CHUNKS,)),
             dma((CHUNKS * 8,)), dma((CHUNKS * 8,)),
-            dma((CHUNKS,)),
         ],
         compiler_params=pltpu.CompilerParams(
             collective_id=0, has_side_effects=True, vmem_limit_bytes=60 * 1024 * 1024

time: 101 us -> 83.8 us (0.83)
  Pallas kernels: 96.9 us -> 79.8 us
    pallas_call x1, Pallas kernels: 96.9 us -> 79.8 us  [body(): pl.pallas_call(kernel, out_shape=(jax.ShapeDtypeStruct((SHARE, INST_DEV),...]
where the time goes in v2:
time: 83.8 us; the launch traced here: 83.5 us
  Pallas kernels  79.8 us (95%)
  local copies, waits for them, and re-layouts  3.08 us (4%)
    pallas_call x1, Pallas kernels, body(): pl.pallas_call(kernel, out_shape=(jax.ShapeDtypeStruct((SHARE, INST_DEV),...  79.8 us

profile of v2, /device:TPU:8, one launch (start us, length us, event | category | flops | bytes accessed | tf_op | source)
XLA Modules:
  0.0 83.5 jit_solution(12731634964269381074)
XLA Ops:
  0.6 79.8 %revalue.1 = (f32[16,4096]{1,0:T(8,128)}, f32[16,1,128]{2,1,0:T(1,128)}) custom-call(bf16[512,128]{1,0:T(8,128)(2,1)} %shocks.1, bf16[2048,4096]{1,0:T(8,128)(2,1)} %loadings.1, f32[1,4096]{1,0:T(1,128)} %bitcast.4, f32[1,4096]{1,0:T(1,128)} %bitcast.5, f32[1,4096]{1,0:T(1,128)} %bitcast.6, s32[1,4096]{1,0:T(1,128)} %bitcast.7, s32[256]{0:T(256)} %low.1, ...), custom_call_target="tpu_custom_call" | custom-call | tf_op jit(solution)/shard_map/revalue/pallas_call | solution.py:436
  80.4 1.4 %slice_reduce_fusion = f32[16]{0:T(128)} fusion(f32[16,1,128]{2,1,0:T(1,128)} %get-tuple-element.5), kind=kLoop, calls=%fused_computation | loop fusion | bytes 128 | tf_op jit(solution)/shard_map/slice | solution.py:484
  81.8 1.7 %copy.12 = f32[16,4096]{1,0:T(8,128)} copy(f32[16,4096]{1,0:T(8,128)} %get-tuple-element.8) | data formatting | bytes 524288

commit v3 on v2

--- a/solution.py
+++ b/solution.py
@@ -24,7 +24,7 @@
 FACT_DEV = 128
 FACTORS = 2048
 INST_DEV = 4096
-TILE = 512
+TILE = 1024
 TILES = INST_DEV // TILE
 CHUNKS = 4
 CHUNK = INST_DEV // CHUNKS
@@ -44,7 +44,7 @@
 def kernel(
     shocks, loadings, delta, gamma, kappa, book_of, low, high, rank,
     out, qout,
-    LH, LD, ACC, PR, OH, SENS, BK, PS, RS, ROWS, DV, PNL, QR, QA, W,
+    LH, LD, ACC, PR, OH, SENS, BK, ST, PS, RS, ROWS, DV, PNL, QR, QA, W,
     SIBS, SIBR, OWNC, RSND, RRCV,
     ld_sem, in_sem, a_send, a_recv, c_send, c_recv, d_send, d_recv, g_send, g_recv,
     f_send, f_recv, sib_send, sib_recv, r_send, r_recv,
@@ -187,11 +187,11 @@
 
     def one_hot(n, carry):
         cols = pl.ds(pl.multiple_of(n * TILE, TILE), TILE)
-        OH[:, cols] = jnp.where(BK[:, cols] == book_ids, 1.0, 0.0).astype(BF16)
+        OH[cols, :] = jnp.transpose(jnp.where(BK[:, cols] == book_ids, 1.0, 0.0).astype(BF16))
         return carry
 
     lax.fori_loop(0, TILES, one_hot, 0)
-    PS[...] = jnp.zeros_like(PS)
+    ST[...] = jnp.zeros_like(ST)
     a_step(1)
     a_step(2)
     for cp in small[:4]:
@@ -201,6 +201,8 @@
         return pl.ds(pl.multiple_of(k * SHARE, SHARE), SHARE)
 
     def send_sums(h):
+        PS[h] = jnp.transpose(ST[h])
+
         def one(k, carry):
             p = inst_peer(k)
             remote(PS.at[h, share_rows(p), :], RS.at[h, i], c_send.at[h], c_recv.at[h], inst=p).start()
@@ -253,7 +255,7 @@
         cols = tile_cols(n)
         ACC[:, cols] += jnp.dot(LH[:, factors(1)], LD[factors(1), cols], preferred_element_type=F32)
 
-        @pl.when(n == 4)
+        @pl.when(n == TILES // 2)
         def _():
             a_step(5)
 
@@ -266,8 +268,7 @@
         d, g, k = SENS[0, :, cols], SENS[1, :, cols], SENS[2, :, cols]
         profit = (moves * (d + moves * (g + moves * k))).astype(BF16)
         PR[rows, cols] = profit
-        part = lax.dot_general(OH[:, cols], profit, (((1,), (1,)), ((), ())), preferred_element_type=F32)
-        PS[h] += part
+        ST[h] += jnp.dot(profit, OH[cols, :], preferred_element_type=F32)
 
     def last_first(n, carry):
         last_group(0, n)
@@ -336,7 +337,9 @@
 
     lax.fori_loop(1, N_INST, send_all_q, 0)
     QA[i] = QR[...]
-    qout[...] = QR[...]
+    books = lax.broadcasted_iota(jnp.int32, (SHARE, 128), 0)
+    lanes_q = lax.broadcasted_iota(jnp.int32, (SHARE, 128), 1)
+    qout[...] = jnp.sum(jnp.where(books == lanes_q, QR[:, 0, :], 0.0), axis=0)[:SHARE]
     for h in range(2):
         drain(PNL.at[pl.ds(0, N_INST - 1), h], g_recv.at[h])
     drain(QA.at[pl.ds(0, N_INST - 1)], f_recv.at[1])
@@ -400,11 +403,16 @@
                     RSND[slot, :, halves[u]] = v.astype(BF16)
             ring_copy(n, way, step).start()
 
+    def first_step(n):
+        sib_copy(n).wait_recv()
+        ring_step(n, 0)
+
     for n in range(CHUNKS):
         contribute(n)
-    for n in range(CHUNKS):
-        sib_copy(n).wait_recv()
-        ring_step(n, 0)
+        if n > 1:
+            first_step(n - 2)
+    first_step(CHUNKS - 2)
+    first_step(CHUNKS - 1)
     for n in range(CHUNKS):
         ring_step(n, 1)
     for n in range(CHUNKS):
@@ -436,8 +444,8 @@
     out, q = pl.pallas_call(
         kernel,
         out_shape=(
-            jax.ShapeDtypeStruct((SHARE, INST_DEV), F32),
-            jax.ShapeDtypeStruct((SHARE, 1, 128), F32),
+            pltpu.VMEM((SHARE, INST_DEV), F32),
+            pltpu.VMEM((SHARE,), F32),
         ),
         in_specs=[anywhere] * 6 + [scalars] * 3,
         out_specs=(pl.BlockSpec(memory_space=pltpu.VMEM),) * 2,
@@ -446,9 +454,10 @@
             pltpu.VMEM((FACTORS, INST_DEV), BF16),
             pltpu.VMEM((SCEN_DEV, INST_DEV), F32),
             pltpu.VMEM((SCEN_DEV, INST_DEV), BF16),
-            pltpu.VMEM((BOOKS, INST_DEV), BF16),
+            pltpu.VMEM((INST_DEV, BOOKS), BF16),
             pltpu.VMEM((3, 1, INST_DEV), F32),
             pltpu.VMEM((1, INST_DEV), jnp.int32),
+            pltpu.VMEM((2, HALF, BOOKS), F32),
             pltpu.VMEM((2, BOOKS, HALF), F32),
             pltpu.VMEM((2, N_INST, SHARE, HALF), F32),
             pltpu.VMEM((2, SHARE, 2, 128), F32),
@@ -481,7 +490,7 @@
         shocks, loadings, row(delta), row(gamma), row(kappa), row(book_of),
         bracket_low, bracket_high, rank,
     )
-    return out, q[:, 0, 0]
+    return out, q
 
 
 def solution(mesh):

time: 83.8 us -> 78.4 us (0.936)
  Pallas kernels: 79.8 us -> 76.3 us
  local copies, waits for them, and re-layouts: 3.08 us -> 1.22 us
    pallas_call x1, Pallas kernels: 79.8 us -> 76.3 us  [body(): pl.pallas_call(kernel, out_shape=(pltpu.VMEM((SHARE, INST_DEV), F32), plt...]
    slice x1 -> x0, local copies, waits for them, and re-layouts: 1.41 us -> none  [body(): return (out, q[:, 0, 0])]
where the time goes in v3:
time: 78.4 us; the launch traced here: 78.2 us
  Pallas kernels  76.3 us (97%)
  local copies, waits for them, and re-layouts  1.22 us (2%)
    pallas_call x1, Pallas kernels, body(): pl.pallas_call(kernel, out_shape=(pltpu.VMEM((SHARE, INST_DEV), F32), plt...  76.3 us

profile of v3, /device:TPU:8, one launch (start us, length us, event | category | flops | bytes accessed | tf_op | source)
XLA Modules:
  0.0 78.2 jit_solution(12550350148269024022)
XLA Ops:
  0.6 76.3 %revalue.1 = (f32[16,4096]{1,0:T(8,128)S(1)}, f32[16]{0:T(128)S(1)}) custom-call(bf16[512,128]{1,0:T(8,128)(2,1)} %shocks.1, bf16[2048,4096]{1,0:T(8,128)(2,1)} %loadings.1, f32[1,4096]{1,0:T(1,128)} %bitcast.4, f32[1,4096]{1,0:T(1,128)} %bitcast.5, f32[1,4096]{1,0:T(1,128)} %bitcast.6, s32[1,4096]{1,0:T(1,128)} %bitcast.7, s32[256]{0:T(256)} %low.1, ...), custom_call_target="tpu_custom_call" | custom-call | tf_op jit(solution)/shard_map/revalue/pallas_call | solution.py:444
  77.0 0.7 copy.13
  77.7 0.5 copy.14

commit v4 on v3

--- a/solution.py
+++ b/solution.py
@@ -42,11 +42,11 @@
 
 
 def kernel(
-    shocks, loadings, delta, gamma, kappa, book_of, low, high, rank,
+    shocks, loadings, delta, gamma, kappa, book_of, low_in, high_in, rank_in,
     out, qout,
-    LH, LD, ACC, PR, OH, SENS, BK, ST, PS, RS, ROWS, DV, PNL, QR, QA, W,
+    low, high, rank, LH, LD, ACC, PR, OH, SENS, BK, ST, PS, RS, ROWS, DV, PNL, QR, QA, W,
     SIBS, SIBR, OWNC, RSND, RRCV,
-    ld_sem, in_sem, a_send, a_recv, c_send, c_recv, d_send, d_recv, g_send, g_recv,
+    word, ld_sem, in_sem, a_send, a_recv, c_send, c_recv, d_send, d_recv, g_send, g_recv,
     f_send, f_recv, sib_send, sib_recv, r_send, r_recv,
 ):
     s = lax.axis_index("scen")
@@ -75,12 +75,29 @@
     def drain(ref, sem):
         pltpu.make_async_copy(ref, ref, sem).wait()
 
+    barrier = pltpu.get_barrier_semaphore()
+    for dx, dy in PLACES[1:5]:
+        pl.semaphore_signal(barrier, inc=1, device_id={"inst": inst_at(dx, dy)}, device_id_type=MESH)
+    up, down, partner = ring_pos(1) * 2 + c, ring_pos(-1) * 2 + c, z * 2 + (1 - c)
+    for peer in (partner, up, down):
+        pl.semaphore_signal(barrier, inc=1, device_id={"scen": peer}, device_id_type=MESH)
+
+    def tell(r):
+        for peer in (up, down):
+            pl.semaphore_signal(word.at[r], inc=1, device_id={"scen": peer}, device_id_type=MESH)
+
+    def hear(r):
+        pl.semaphore_wait(word.at[r], 2)
+
     small = [
         pltpu.make_async_copy(shocks, LH.at[:, pl.ds(0, FACT_DEV)], in_sem.at[0]),
         pltpu.make_async_copy(delta, SENS.at[0], in_sem.at[1]),
         pltpu.make_async_copy(gamma, SENS.at[1], in_sem.at[2]),
         pltpu.make_async_copy(kappa, SENS.at[2], in_sem.at[3]),
         pltpu.make_async_copy(book_of, BK, in_sem.at[4]),
+        pltpu.make_async_copy(low_in, low, in_sem.at[5]),
+        pltpu.make_async_copy(high_in, high, in_sem.at[6]),
+        pltpu.make_async_copy(rank_in, rank, in_sem.at[7]),
     ]
     for cp in small:
         cp.start()
@@ -96,15 +113,7 @@
     for p in range(N_INST):
         load_block(p).start()
 
-    barrier = pltpu.get_barrier_semaphore()
-
-    def greet(k, carry):
-        pl.semaphore_signal(barrier, inc=1, device_id={"inst": inst_peer(k)}, device_id_type=MESH)
-        pl.semaphore_signal(barrier, inc=1, device_id={"scen": scen_peer(k)}, device_id_type=MESH)
-        return carry
-
-    lax.fori_loop(1, 16, greet, 0)
-    pl.semaphore_wait(barrier, 30)
+    pl.semaphore_wait(barrier, 7)
 
     def along(colour, first, second):
         return inst_at(first, second) if colour == 0 else inst_at(second, first)
@@ -182,6 +191,7 @@
                     a_last(colour, q)
 
     a_step(0)
+    tell(0)
     small[4].wait()
     book_ids = lax.broadcasted_iota(jnp.int32, (BOOKS, TILE), 0)
 
@@ -193,8 +203,10 @@
     lax.fori_loop(0, TILES, one_hot, 0)
     ST[...] = jnp.zeros_like(ST)
     a_step(1)
+    hear(0)
+    tell(1)
     a_step(2)
-    for cp in small[:4]:
+    for cp in small[:4] + small[5:]:
         cp.wait()
 
     def share_rows(k):
@@ -228,13 +240,15 @@
 
         lax.fori_loop(1, N_SCEN, one, 0)
 
-        def other(k, carry):
+        DV[h, s] = ROWS[h, s]
+
+    def share_sums(h):
+        def one(k, carry):
             p = inst_peer(k)
             remote(PNL.at[i, h], PNL.at[i, h], g_send.at[h], g_recv.at[h], inst=p).start()
             return carry
 
-        lax.fori_loop(1, N_INST, other, 0)
-        DV[h, s] = ROWS[h, s]
+        lax.fori_loop(1, N_INST, one, 0)
 
     def factors(group):
         return pl.ds(CUTS[group] * FACT_DEV, (CUTS[group + 1] - CUTS[group]) * FACT_DEV)
@@ -280,18 +294,25 @@
 
     wait_blocks(0)
     lax.fori_loop(0, TILES, first_group, 0)
+    hear(1)
+    tell(2)
     a_step(3)
     a_step(4)
     wait_blocks(1)
     lax.fori_loop(0, TILES, second_group, 0)
+    hear(2)
+    tell(3)
     a_step(6)
     wait_blocks(2)
+    hear(3)
     lax.fori_loop(0, TILES, last_first, 0)
     send_sums(0)
     lax.fori_loop(0, TILES, last_second, 0)
     send_sums(1)
     take_sums(0)
     take_sums(1)
+    share_sums(0)
+    share_sums(1)
 
     book = i * SHARE + s
     lower = jnp.full((PIVOTS, 128), low[book], jnp.int32).astype(F32) * 0.125
@@ -345,7 +366,9 @@
     drain(QA.at[pl.ds(0, N_INST - 1)], f_recv.at[1])
 
     for t in range(N_INST):
-        place = jnp.where(c == t % 2, BOOKS // 2, 0) + (t // 2) * SHARE
+        ahead = lax.rem(t // 2 - z + RING, RING)
+        order = jnp.where(ahead == 0, 7, jnp.where(ahead < 4, 7 - 2 * ahead, 2 * ahead - 8))
+        place = jnp.where(c == t % 2, BOOKS // 2, 0) + order * SHARE
         q = QA[t, :, 0, :][:, 0:1]
         for h in range(2):
             w = sigmoid((q - PNL[t, h]) * 2.0).astype(BF16)
@@ -353,16 +376,23 @@
 
     own_mass = QA[s, :, 0, :][:, 64:65]
 
-    def sib_copy(n):
-        return remote(SIBS.at[n], SIBR.at[n], sib_send.at[n], sib_recv.at[n], scen=z * 2 + (1 - c))
+    def chunk_cols(n):
+        return pl.ds(n * CHUNK, CHUNK)
+
+    def sib_copy(k):
+        if k < CHUNKS:
+            part = (pl.ds(0, SHARE), chunk_cols(k))
+        else:
+            start, size = ((1, 2), (3, 2), (5, 3))[k - CHUNKS]
+            part = (pl.ds(start * SHARE, size * SHARE), pl.ds(0, INST_DEV))
+        return remote(SIBS.at[part], SIBR.at[part], sib_send.at[k], sib_recv.at[k], scen=partner)
 
     def contribute(n):
         for u in range(2):
-            width = CHUNK // 2
-            cols = pl.ds(n * CHUNK + u * width, width)
+            cols = pl.ds(n * CHUNK + u * (CHUNK // 2), CHUNK // 2)
             both = jnp.dot(W[...], PR[:, cols], preferred_element_type=F32)
-            SIBS[n, :, pl.ds(u * width, width)] = both[: BOOKS // 2].astype(BF16)
-            OWNC[n, :, pl.ds(u * width, width)] = both[BOOKS // 2 :]
+            SIBS[:, cols] = both[: BOOKS // 2].astype(BF16)
+            OWNC[:, cols] = both[BOOKS // 2 :]
         sib_copy(n).start()
 
     def ring_copy(n, way, step):
@@ -373,50 +403,51 @@
         slot = (n * 2 + way) * 4 + step
         return remote(
             RSND.at[slot, :, cols], RRCV.at[slot, :, cols], r_send.at[slot], r_recv.at[slot],
-            scen=ring_pos(1 if way == 0 else -1) * 2 + c,
+            scen=up if way == 0 else down,
         )
 
-    def held(n, dest, cols):
-        rows = pl.ds(pl.multiple_of(dest * SHARE, SHARE), SHARE)
-        return OWNC[n, rows, cols] + SIBR[n, rows, cols].astype(F32)
+    def held(n, step, way, u, count):
+        order = 0 if step == 0 else 7 if step == 4 else 2 * step - 1 + way
+        rows = pl.ds(order * SHARE, SHARE)
+        cols = pl.ds(n * CHUNK + u * (CHUNK // 2), count * (CHUNK // 2))
+        return OWNC[rows, cols] + SIBR[rows, cols].astype(F32)
 
     def ring_step(n, step):
         halves = (pl.ds(0, CHUNK // 2), pl.ds(CHUNK // 2, CHUNK // 2))
         if step == 4:
             ring_copy(n, 0, 3).wait_recv()
             ring_copy(n, 1, 3).wait_recv()
-            total = held(n, z, pl.ds(0, CHUNK))
+            total = held(n, 4, 0, 0, 2)
             total = total + RRCV[(n * 2) * 4 + 3].astype(F32) + RRCV[(n * 2 + 1) * 4 + 3].astype(F32)
-            out[:, pl.ds(n * CHUNK, CHUNK)] = total / own_mass
+            out[:, chunk_cols(n)] = total / own_mass
             return
         for way in range(2):
             slot = (n * 2 + way) * 4 + step
-            dest = ring_pos((4 - step) * (1 if way == 0 else -1))
             if step == 0:
-                RSND[slot, :, halves[way]] = held(n, dest, halves[way]).astype(BF16)
+                RSND[slot, :, halves[way]] = held(n, 0, way, way, 1).astype(BF16)
             else:
                 ring_copy(n, way, step - 1).wait_recv()
                 for u in range(2):
-                    v = held(n, dest, halves[u])
+                    v = held(n, step, way, u, 1)
                     if step > 1 or u == way:
                         v = v + RRCV[slot - 1, :, halves[u]].astype(F32)
                     RSND[slot, :, halves[u]] = v.astype(BF16)
             ring_copy(n, way, step).start()
 
-    def first_step(n):
+    for n in range(CHUNKS):
+        contribute(n)
+    for k in range(CHUNKS, CHUNKS + 3):
+        sib_copy(k).start()
+    for n in range(CHUNKS):
         sib_copy(n).wait_recv()
         ring_step(n, 0)
-
-    for n in range(CHUNKS):
-        contribute(n)
-        if n > 1:
-            first_step(n - 2)
-    first_step(CHUNKS - 2)
-    first_step(CHUNKS - 1)
+    sib_copy(CHUNKS).wait_recv()
     for n in range(CHUNKS):
         ring_step(n, 1)
+    sib_copy(CHUNKS + 1).wait_recv()
     for n in range(CHUNKS):
         ring_step(n, 2)
+    sib_copy(CHUNKS + 2).wait_recv()
     for n in range(CHUNKS):
         ring_step(n, 3)
     for n in range(CHUNKS):
@@ -429,8 +460,9 @@
         drain(PNL.at[pl.ds(0, N_INST - 1), h], g_send.at[h])
     drain(QR.at[pl.ds(0, N_SCEN - 1)], f_send.at[0])
     drain(QA.at[pl.ds(0, N_INST - 1)], f_send.at[1])
-    for n in range(CHUNKS):
-        sib_copy(n).wait_send()
+    for k in range(CHUNKS + 3):
+        sib_copy(k).wait_send()
+    for n in range(CHUNKS):
         for way in range(2):
             for step in range(4):
                 ring_copy(n, way, step).wait_send()
@@ -438,7 +470,6 @@
 
 def body(shocks, loadings, delta, gamma, kappa, book_of, bracket_low, bracket_high, rank):
     anywhere = pl.BlockSpec(memory_space=pl.ANY)
-    scalars = pl.BlockSpec(memory_space=pltpu.SMEM)
     row = lambda v: v.reshape(1, INST_DEV)
     dma = pltpu.SemaphoreType.DMA
     out, q = pl.pallas_call(
@@ -447,9 +478,12 @@
             pltpu.VMEM((SHARE, INST_DEV), F32),
             pltpu.VMEM((SHARE,), F32),
         ),
-        in_specs=[anywhere] * 6 + [scalars] * 3,
+        in_specs=[anywhere] * 9,
         out_specs=(pl.BlockSpec(memory_space=pltpu.VMEM),) * 2,
         scratch_shapes=[
+            pltpu.SMEM((BOOKS,), jnp.int32),
+            pltpu.SMEM((BOOKS,), jnp.int32),
+            pltpu.SMEM((BOOKS,), jnp.int32),
             pltpu.VMEM((SCEN_DEV, FACTORS), BF16),
             pltpu.VMEM((FACTORS, INST_DEV), BF16),
             pltpu.VMEM((SCEN_DEV, INST_DEV), F32),
@@ -466,20 +500,21 @@
             pltpu.VMEM((SHARE, 1, 128), F32),
             pltpu.VMEM((N_INST, SHARE, 1, 128), F32),
             pltpu.VMEM((BOOKS, SCEN_DEV), BF16),
-            pltpu.VMEM((CHUNKS, BOOKS // 2, CHUNK), BF16),
-            pltpu.VMEM((CHUNKS, BOOKS // 2, CHUNK), BF16),
-            pltpu.VMEM((CHUNKS, BOOKS // 2, CHUNK), F32),
+            pltpu.VMEM((BOOKS // 2, INST_DEV), BF16),
+            pltpu.VMEM((BOOKS // 2, INST_DEV), BF16),
+            pltpu.VMEM((BOOKS // 2, INST_DEV), F32),
             pltpu.VMEM((CHUNKS * 8, SHARE, CHUNK), BF16),
             pltpu.VMEM((CHUNKS * 8, SHARE, CHUNK), BF16),
+            pltpu.SemaphoreType.REGULAR((4,)),
             dma((N_INST,)),
-            dma((5,)),
+            dma((8,)),
             dma(()),
             dma((40,)),
             dma((2,)), dma((2,)),
             dma((2,)), dma((2,)),
             dma((2,)), dma((2,)),
             dma((2,)), dma((2,)),
-            dma((CHUNKS,)), dma((CHUNKS,)),
+            dma((CHUNKS + 3,)), dma((CHUNKS + 3,)),
             dma((CHUNKS * 8,)), dma((CHUNKS * 8,)),
         ],
         compiler_params=pltpu.CompilerParams(

time: 78.4 us -> 75.9 us (0.968)
  Pallas kernels: 76.3 us -> 73.9 us
    pallas_call x1, Pallas kernels: 76.3 us -> 73.9 us  [body(): pl.pallas_call(kernel, out_shape=(pltpu.VMEM((SHARE, INST_DEV), F32), plt...]
where the time goes in v4:
time: 75.9 us; the launch traced here: 75.8 us
  Pallas kernels  73.9 us (97%)
  local copies, waits for them, and re-layouts  1.22 us (2%)
    pallas_call x1, Pallas kernels, body(): pl.pallas_call(kernel, out_shape=(pltpu.VMEM((SHARE, INST_DEV), F32), plt...  73.9 us

profile of v4, /device:TPU:8, one launch (start us, length us, event | category | flops | bytes accessed | tf_op | source)
XLA Modules:
  0.0 75.8 jit_solution(13005726902334563607)
XLA Ops:
  0.6 73.9 %revalue.1 = (f32[16,4096]{1,0:T(8,128)S(1)}, f32[16]{0:T(128)S(1)}) custom-call(bf16[512,128]{1,0:T(8,128)(2,1)} %shocks.1, bf16[2048,4096]{1,0:T(8,128)(2,1)} %loadings.1, f32[1,4096]{1,0:T(1,128)} %bitcast.4, f32[1,4096]{1,0:T(1,128)} %bitcast.5, f32[1,4096]{1,0:T(1,128)} %bitcast.6, s32[1,4096]{1,0:T(1,128)} %bitcast.7, s32[256]{0:T(256)} %low_in.1, ...), custom_call_target="tpu_custom_call" | custom-call | tf_op jit(solution)/shard_map/revalue/pallas_call | solution.py:475
  74.6 0.7 copy.13
  75.3 0.5 copy.14

commit v5 on v4

--- a/solution.py
+++ b/solution.py
@@ -33,7 +33,7 @@
     (-1, -1), (-1, 1), (1, -1), (1, 1), (2, 0), (0, 2),
     (2, -1), (2, 1), (-1, 2), (1, 2), (2, 2),
 )
-CUTS = (0, 4, 10, 16)
+CUTS = (0, 4, 10, 14, 16)
 SCALE = (BOOKS / (INST_DEV * N_INST)) ** 0.5
 
 
@@ -57,11 +57,11 @@
     def inst_at(dx, dy):
         return lax.rem(x + dx + SIDE, SIDE) * SIDE + lax.rem(y + dy + SIDE, SIDE)
 
-    def inst_peer(k):
-        return lax.rem(i + k, N_INST)
-
-    def scen_peer(k):
-        return lax.rem(s + k, N_SCEN)
+    def inst_peers():
+        return [inst_at(dx, dy) for dx, dy in PLACES[:0:-1]]
+
+    def scen_peers():
+        return [lax.rem(s + k, N_SCEN) for k in sorted(range(1, N_SCEN), key=lambda k: abs(k - N_SCEN // 2))]
 
     def ring_pos(d):
         return lax.rem(z + d + RING, RING)
@@ -90,7 +90,7 @@
         pl.semaphore_wait(word.at[r], 2)
 
     small = [
-        pltpu.make_async_copy(shocks, LH.at[:, pl.ds(0, FACT_DEV)], in_sem.at[0]),
+        pltpu.make_async_copy(shocks, LH.at[0], in_sem.at[0]),
         pltpu.make_async_copy(delta, SENS.at[0], in_sem.at[1]),
         pltpu.make_async_copy(gamma, SENS.at[1], in_sem.at[2]),
         pltpu.make_async_copy(kappa, SENS.at[2], in_sem.at[3]),
@@ -110,8 +110,11 @@
             ld_sem.at[p],
         )
 
-    for p in range(N_INST):
-        load_block(p).start()
+    def start_blocks(group):
+        for p in range(CUTS[group], CUTS[group + 1]):
+            load_block(p).start()
+
+    start_blocks(0)
 
     pl.semaphore_wait(barrier, 7)
 
@@ -122,75 +125,79 @@
         fold = lambda v: (v + 1) % SIDE - 1
         return PLACES.index((fold(a), fold(b)) if colour == 0 else (fold(b), fold(a)))
 
-    def rows_of(colour, part):
-        start, size = colour * HALF, HALF
+    def rows_of(colour, h, part):
+        size = HALF // 2
+        start = colour * HALF + h * size
         if part:
             size //= 2
             start += size * (part - 1)
         return pl.ds(start, size)
 
-    def piece(colour, a, b, part):
-        return LH.at[rows_of(colour, part), pl.ds(place_of(colour, a, b) * FACT_DEV, FACT_DEV)]
-
-    def a_pass(colour, a, b, part, first, second, pid):
+    def piece(colour, h, a, b, part):
+        return LH.at[place_of(colour, a, b), rows_of(colour, h, part), :]
+
+    def a_pass(colour, h, a, b, part, first, second, pid):
         if (a, b) == (0, 0):
-            src = shocks.at[rows_of(colour, part), :]
+            src = shocks.at[rows_of(colour, h, part), :]
         else:
-            src = piece(colour, a, b, part)
+            src = piece(colour, h, a, b, part)
         remote(
-            src, piece(colour, a - first, b - second, part), a_send, a_recv.at[colour * 20 + pid],
+            src, piece(colour, h, a - first, b - second, part), a_send, a_recv.at[(h * 2 + colour) * 20 + pid],
             inst=along(colour, first, second),
         ).start()
 
-    def a_wait(colour, a, b, part, pid):
-        drain(piece(colour, a, b, part), a_recv.at[colour * 20 + pid])
+    def a_wait(colour, h, a, b, part, pid):
+        drain(piece(colour, h, a, b, part), a_recv.at[(h * 2 + colour) * 20 + pid])
 
     lanes = (0, -1, 1, 2)
 
-    def a_second(colour, q):
-        a_pass(colour, lanes[q], 0, 0, 0, 1, 4 + 4 * q)
-        a_pass(colour, lanes[q], 0, 0, 0, -1, 5 + 4 * q)
-
-    def a_hand_on(colour, q):
-        a_wait(colour, lanes[q], -1, 0, 4 + 4 * q)
-        a_pass(colour, lanes[q], -1, 1, 0, 1, 6 + 4 * q)
-        a_wait(colour, lanes[q], 1, 0, 5 + 4 * q)
-        a_pass(colour, lanes[q], 1, 2, 0, -1, 7 + 4 * q)
-
-    def a_last(colour, q):
-        a_wait(colour, lanes[q], 2, 1, 6 + 4 * q)
-        a_wait(colour, lanes[q], 2, 2, 7 + 4 * q)
-
-    def a_step(step):
+    def a_second(colour, h, q):
+        a_pass(colour, h, lanes[q], 0, 0, 0, 1, 4 + 4 * q)
+        a_pass(colour, h, lanes[q], 0, 0, 0, -1, 5 + 4 * q)
+
+    def a_hand_on(colour, h, q):
+        a_wait(colour, h, lanes[q], -1, 0, 4 + 4 * q)
+        a_pass(colour, h, lanes[q], -1, 1, 0, 1, 6 + 4 * q)
+        a_wait(colour, h, lanes[q], 1, 0, 5 + 4 * q)
+        a_pass(colour, h, lanes[q], 1, 2, 0, -1, 7 + 4 * q)
+
+    def a_last(colour, h, q):
+        a_wait(colour, h, lanes[q], 2, 1, 6 + 4 * q)
+        a_wait(colour, h, lanes[q], 2, 2, 7 + 4 * q)
+
+    def a_step(h, step):
         for colour in range(2):
             if step == 0:
-                a_pass(colour, 0, 0, 0, 1, 0, 0)
-                a_pass(colour, 0, 0, 0, -1, 0, 1)
-                a_second(colour, 0)
+                a_pass(colour, h, 0, 0, 0, 1, 0, 0)
+                a_pass(colour, h, 0, 0, 0, -1, 0, 1)
+                a_second(colour, h, 0)
             elif step == 1:
-                a_wait(colour, -1, 0, 0, 0)
-                a_pass(colour, -1, 0, 1, 1, 0, 2)
-                a_second(colour, 1)
-                a_wait(colour, 1, 0, 0, 1)
-                a_pass(colour, 1, 0, 2, -1, 0, 3)
-                a_second(colour, 2)
+                a_wait(colour, h, -1, 0, 0, 0)
+                a_pass(colour, h, -1, 0, 1, 1, 0, 2)
+                a_second(colour, h, 1)
+                a_wait(colour, h, 1, 0, 0, 1)
+                a_pass(colour, h, 1, 0, 2, -1, 0, 3)
+                a_second(colour, h, 2)
             elif step == 2:
-                a_hand_on(colour, 0)
+                a_hand_on(colour, h, 0)
             elif step == 3:
-                a_wait(colour, 2, 0, 1, 2)
-                a_wait(colour, 2, 0, 2, 3)
-                a_second(colour, 3)
+                a_wait(colour, h, 2, 0, 1, 2)
+                a_wait(colour, h, 2, 0, 2, 3)
+                a_second(colour, h, 3)
             elif step == 4:
-                a_hand_on(colour, 1)
-                a_hand_on(colour, 2)
-                a_last(colour, 0)
+                a_hand_on(colour, h, 1)
+                a_hand_on(colour, h, 2)
+                a_last(colour, h, 0)
             elif step == 5:
-                a_hand_on(colour, 3)
+                a_hand_on(colour, h, 3)
+            elif step == 6:
+                a_last(colour, h, 1)
+                a_last(colour, h, 2)
             else:
-                for q in range(1, 4):
-                    a_last(colour, q)
-
-    a_step(0)
+                a_last(colour, h, 3)
+
+    a_step(0, 0)
+    a_step(1, 0)
     tell(0)
     small[4].wait()
     book_ids = lax.broadcasted_iota(jnp.int32, (BOOKS, TILE), 0)
@@ -201,11 +208,16 @@
         return carry
 
     lax.fori_loop(0, TILES, one_hot, 0)
+    start_blocks(1)
     ST[...] = jnp.zeros_like(ST)
-    a_step(1)
+    a_step(0, 1)
+    a_step(0, 2)
+    a_step(1, 1)
+    a_step(1, 2)
+    start_blocks(2)
+    start_blocks(3)
     hear(0)
     tell(1)
-    a_step(2)
     for cp in small[:4] + small[5:]:
         cp.wait()
 
@@ -215,12 +227,8 @@
     def send_sums(h):
         PS[h] = jnp.transpose(ST[h])
 
-        def one(k, carry):
-            p = inst_peer(k)
+        for p in inst_peers():
             remote(PS.at[h, share_rows(p), :], RS.at[h, i], c_send.at[h], c_recv.at[h], inst=p).start()
-            return carry
-
-        lax.fori_loop(1, N_INST, one, 0)
         RS[h, i] = PS[h, share_rows(i), :]
 
     def take_sums(h):
@@ -233,25 +241,20 @@
         for r in range(2):
             ROWS[h, :, r, :] = total[:, r * 128 : (r + 1) * 128]
 
-        def one(k, carry):
-            p = scen_peer(k)
+        for p in scen_peers():
             remote(ROWS.at[h, p], DV.at[h, s], d_send.at[h], d_recv.at[h], scen=p).start()
-            return carry
-
-        lax.fori_loop(1, N_SCEN, one, 0)
 
         DV[h, s] = ROWS[h, s]
 
     def share_sums(h):
-        def one(k, carry):
-            p = inst_peer(k)
+        for p in inst_peers():
             remote(PNL.at[i, h], PNL.at[i, h], g_send.at[h], g_recv.at[h], inst=p).start()
-            return carry
-
-        lax.fori_loop(1, N_INST, one, 0)
 
     def factors(group):
         return pl.ds(CUTS[group] * FACT_DEV, (CUTS[group + 1] - CUTS[group]) * FACT_DEV)
+
+    def scenarios(group, rows):
+        return jnp.concatenate([LH[p, rows, :] for p in range(CUTS[group], CUTS[group + 1])], axis=1)
 
     def wait_blocks(group):
         for p in range(CUTS[group], CUTS[group + 1]):
@@ -262,23 +265,35 @@
 
     def first_group(n, carry):
         cols = tile_cols(n)
-        ACC[:, cols] = jnp.dot(LH[:, factors(0)], LD[factors(0), cols], preferred_element_type=F32)
+        ACC[:, cols] = jnp.dot(scenarios(0, slice(None)), LD[factors(0), cols], preferred_element_type=F32)
+
+        @pl.when(n == TILES - 1)
+        def _():
+            a_step(0, 3)
+            a_step(0, 4)
+
         return carry
 
     def second_group(n, carry):
         cols = tile_cols(n)
-        ACC[:, cols] += jnp.dot(LH[:, factors(1)], LD[factors(1), cols], preferred_element_type=F32)
-
-        @pl.when(n == TILES // 2)
-        def _():
-            a_step(5)
-
+        ACC[:, cols] += jnp.dot(scenarios(1, slice(None)), LD[factors(1), cols], preferred_element_type=F32)
+
+        for h in range(2):
+            @pl.when(n == TILES // 2 + h)
+            def _():
+                a_step(h, 5)
+
+        return carry
+
+    def third_group(n, carry):
+        cols = tile_cols(n)
+        ACC[:, cols] += jnp.dot(scenarios(2, slice(None)), LD[factors(2), cols], preferred_element_type=F32)
         return carry
 
     def last_group(h, n):
         cols = tile_cols(n)
         rows = pl.ds(h * HALF, HALF)
-        moves = ACC[rows, cols] + jnp.dot(LH[rows, factors(2)], LD[factors(2), cols], preferred_element_type=F32)
+        moves = ACC[rows, cols] + jnp.dot(scenarios(3, rows), LD[factors(3), cols], preferred_element_type=F32)
         d, g, k = SENS[0, :, cols], SENS[1, :, cols], SENS[2, :, cols]
         profit = (moves * (d + moves * (g + moves * k))).astype(BF16)
         PR[rows, cols] = profit
@@ -296,14 +311,19 @@
     lax.fori_loop(0, TILES, first_group, 0)
     hear(1)
     tell(2)
-    a_step(3)
-    a_step(4)
+    a_step(1, 3)
+    a_step(1, 4)
     wait_blocks(1)
     lax.fori_loop(0, TILES, second_group, 0)
     hear(2)
     tell(3)
-    a_step(6)
+    for h in range(2):
+        a_step(h, 6)
     wait_blocks(2)
+    lax.fori_loop(0, TILES, third_group, 0)
+    for h in range(2):
+        a_step(h, 7)
+    wait_blocks(3)
     hear(3)
     lax.fori_loop(0, TILES, last_first, 0)
     send_sums(0)
@@ -345,22 +365,22 @@
     lane = lax.broadcasted_iota(jnp.int32, (1, 128), 1)
     QR[s] = jnp.where(lane < 64, quantile[0:1, :], jnp.broadcast_to(mass, (1, 128)))
 
-    def send_q(k, carry):
-        remote(QR.at[s], QR.at[s], f_send.at[0], f_recv.at[0], scen=scen_peer(k)).start()
-        return carry
-
-    lax.fori_loop(1, N_SCEN, send_q, 0)
+    for p in scen_peers():
+        remote(QR.at[s], QR.at[s], f_send.at[0], f_recv.at[0], scen=p).start()
     drain(QR.at[pl.ds(0, N_SCEN - 1)], f_recv.at[0])
 
-    def send_all_q(k, carry):
-        remote(QR, QA.at[i], f_send.at[1], f_recv.at[1], inst=inst_peer(k)).start()
-        return carry
-
-    lax.fori_loop(1, N_INST, send_all_q, 0)
-    QA[i] = QR[...]
-    books = lax.broadcasted_iota(jnp.int32, (SHARE, 128), 0)
-    lanes_q = lax.broadcasted_iota(jnp.int32, (SHARE, 128), 1)
-    qout[...] = jnp.sum(jnp.where(books == lanes_q, QR[:, 0, :], 0.0), axis=0)[:SHARE]
+    line = lax.broadcasted_iota(jnp.int32, (SHARE, 128), 0)
+    lane = lax.broadcasted_iota(jnp.int32, (SHARE, 128), 1)
+    at_q, at_mass = lane == line, lane == line + 64
+    row_q = jnp.sum(jnp.where(at_q | at_mass, QR[:, 0, :], 0.0), axis=0, keepdims=True)
+    QA[i] = row_q
+    for p in inst_peers():
+        remote(QA.at[i], QA.at[i], f_send.at[1], f_recv.at[1], inst=p).start()
+    qout[...] = row_q[0, :SHARE]
+
+    def column(t, where):
+        return jnp.sum(jnp.where(where, jnp.broadcast_to(QA[t], (SHARE, 128)), 0.0), axis=1, keepdims=True)
+
     for h in range(2):
         drain(PNL.at[pl.ds(0, N_INST - 1), h], g_recv.at[h])
     drain(QA.at[pl.ds(0, N_INST - 1)], f_recv.at[1])
@@ -369,12 +389,12 @@
         ahead = lax.rem(t // 2 - z + RING, RING)
         order = jnp.where(ahead == 0, 7, jnp.where(ahead < 4, 7 - 2 * ahead, 2 * ahead - 8))
         place = jnp.where(c == t % 2, BOOKS // 2, 0) + order * SHARE
-        q = QA[t, :, 0, :][:, 0:1]
+        q = column(t, at_q)
         for h in range(2):
             w = sigmoid((q - PNL[t, h]) * 2.0).astype(BF16)
             W[pl.ds(pl.multiple_of(place, SHARE), SHARE), pl.ds(h * HALF, HALF)] = w
 
-    own_mass = QA[s, :, 0, :][:, 64:65]
+    own_mass = column(s, at_mass)
 
     def chunk_cols(n):
         return pl.ds(n * CHUNK, CHUNK)
@@ -382,8 +402,10 @@
     def sib_copy(k):
         if k < CHUNKS:
             part = (pl.ds(0, SHARE), chunk_cols(k))
+        elif k < 2 * CHUNKS:
+            part = (pl.ds(SHARE, 2 * SHARE), chunk_cols(k - CHUNKS))
         else:
-            start, size = ((1, 2), (3, 2), (5, 3))[k - CHUNKS]
+            start, size = ((3, 2), (5, 3))[k - 2 * CHUNKS]
             part = (pl.ds(start * SHARE, size * SHARE), pl.ds(0, INST_DEV))
         return remote(SIBS.at[part], SIBR.at[part], sib_send.at[k], sib_recv.at[k], scen=partner)
 
@@ -394,6 +416,7 @@
             SIBS[:, cols] = both[: BOOKS // 2].astype(BF16)
             OWNC[:, cols] = both[BOOKS // 2 :]
         sib_copy(n).start()
+        sib_copy(CHUNKS + n).start()
 
     def ring_copy(n, way, step):
         if step == 0:
@@ -434,33 +457,36 @@
                     RSND[slot, :, halves[u]] = v.astype(BF16)
             ring_copy(n, way, step).start()
 
-    for n in range(CHUNKS):
-        contribute(n)
-    for k in range(CHUNKS, CHUNKS + 3):
-        sib_copy(k).start()
-    for n in range(CHUNKS):
+    def first_step(n):
         sib_copy(n).wait_recv()
         ring_step(n, 0)
-    sib_copy(CHUNKS).wait_recv()
-    for n in range(CHUNKS):
+
+    for n in range(CHUNKS):
+        contribute(n)
+    for k in range(2):
+        sib_copy(2 * CHUNKS + k).start()
+    for n in range(CHUNKS):
+        first_step(n)
+    for n in range(CHUNKS):
+        sib_copy(CHUNKS + n).wait_recv()
         ring_step(n, 1)
-    sib_copy(CHUNKS + 1).wait_recv()
+    sib_copy(2 * CHUNKS).wait_recv()
     for n in range(CHUNKS):
         ring_step(n, 2)
-    sib_copy(CHUNKS + 2).wait_recv()
+    sib_copy(2 * CHUNKS + 1).wait_recv()
     for n in range(CHUNKS):
         ring_step(n, 3)
     for n in range(CHUNKS):
         ring_step(n, 4)
 
-    drain(LH.at[pl.ds(0, SCEN_DEV * 15 // 16), :], a_send)
+    drain(LH.at[pl.ds(0, N_INST - 1)], a_send)
     for h in range(2):
         drain(RS.at[h, pl.ds(0, N_INST - 1)], c_send.at[h])
         drain(DV.at[h, pl.ds(0, N_SCEN - 1)], d_send.at[h])
         drain(PNL.at[pl.ds(0, N_INST - 1), h], g_send.at[h])
     drain(QR.at[pl.ds(0, N_SCEN - 1)], f_send.at[0])
     drain(QA.at[pl.ds(0, N_INST - 1)], f_send.at[1])
-    for k in range(CHUNKS + 3):
+    for k in range(2 * CHUNKS + 2):
         sib_copy(k).wait_send()
     for n in range(CHUNKS):
         for way in range(2):
@@ -484,7 +510,7 @@
             pltpu.SMEM((BOOKS,), jnp.int32),
             pltpu.SMEM((BOOKS,), jnp.int32),
             pltpu.SMEM((BOOKS,), jnp.int32),
-            pltpu.VMEM((SCEN_DEV, FACTORS), BF16),
+            pltpu.VMEM((N_INST, SCEN_DEV, FACT_DEV), BF16),
             pltpu.VMEM((FACTORS, INST_DEV), BF16),
             pltpu.VMEM((SCEN_DEV, INST_DEV), F32),
             pltpu.VMEM((SCEN_DEV, INST_DEV), BF16),
@@ -498,7 +524,7 @@
             pltpu.VMEM((2, N_SCEN, 2, 128), F32),
             pltpu.VMEM((N_INST, 2, SHARE, HALF), F32),
             pltpu.VMEM((SHARE, 1, 128), F32),
-            pltpu.VMEM((N_INST, SHARE, 1, 128), F32),
+            pltpu.VMEM((N_INST, 1, 128), F32),
             pltpu.VMEM((BOOKS, SCEN_DEV), BF16),
             pltpu.VMEM((BOOKS // 2, INST_DEV), BF16),
             pltpu.VMEM((BOOKS // 2, INST_DEV), BF16),
@@ -509,12 +535,12 @@
             dma((N_INST,)),
             dma((8,)),
             dma(()),
-            dma((40,)),
+            dma((80,)),
             dma((2,)), dma((2,)),
             dma((2,)), dma((2,)),
             dma((2,)), dma((2,)),
             dma((2,)), dma((2,)),
-            dma((CHUNKS + 3,)), dma((CHUNKS + 3,)),
+            dma((2 * CHUNKS + 2,)), dma((2 * CHUNKS + 2,)),
             dma((CHUNKS * 8,)), dma((CHUNKS * 8,)),
         ],
         compiler_params=pltpu.CompilerParams(

time: 75.9 us -> 72.2 us (0.951)
  Pallas kernels: 73.9 us -> 70.3 us
    pallas_call x1, Pallas kernels: 73.9 us -> 70.3 us  [body(): pl.pallas_call(kernel, out_shape=(pltpu.VMEM((SHARE, INST_DEV), F32), plt...]
where the time goes in v5:
time: 72.2 us; the launch traced here: 72.1 us
  Pallas kernels  70.3 us (97%)
  local copies, waits for them, and re-layouts  1.22 us (2%)
    pallas_call x1, Pallas kernels, body(): pl.pallas_call(kernel, out_shape=(pltpu.VMEM((SHARE, INST_DEV), F32), plt...  70.3 us

profile of v5, /device:TPU:8, one launch (start us, length us, event | category | flops | bytes accessed | tf_op | source)
XLA Modules:
  0.0 72.1 jit_solution(15081839470609619583)
XLA Ops:
  0.6 70.3 %revalue.1 = (f32[16,4096]{1,0:T(8,128)S(1)}, f32[16]{0:T(128)S(1)}) custom-call(bf16[512,128]{1,0:T(8,128)(2,1)} %shocks.1, bf16[2048,4096]{1,0:T(8,128)(2,1)} %loadings.1, f32[1,4096]{1,0:T(1,128)} %bitcast.4, f32[1,4096]{1,0:T(1,128)} %bitcast.5, f32[1,4096]{1,0:T(1,128)} %bitcast.6, s32[1,4096]{1,0:T(1,128)} %bitcast.7, s32[256]{0:T(256)} %low_in.1, ...), custom_call_target="tpu_custom_call" | custom-call | tf_op jit(solution)/shard_map/revalue/pallas_call | solution.py:501
  70.9 0.7 copy.13
  71.6 0.5 copy.14

commit v6 on v5

--- a/solution.py
+++ b/solution.py
@@ -24,7 +24,7 @@
 FACT_DEV = 128
 FACTORS = 2048
 INST_DEV = 4096
-TILE = 1024
+TILE = 2048
 TILES = INST_DEV // TILE
 CHUNKS = 4
 CHUNK = INST_DEV // CHUNKS
@@ -278,10 +278,10 @@
         cols = tile_cols(n)
         ACC[:, cols] += jnp.dot(scenarios(1, slice(None)), LD[factors(1), cols], preferred_element_type=F32)
 
-        for h in range(2):
-            @pl.when(n == TILES // 2 + h)
-            def _():
-                a_step(h, 5)
+        @pl.when(n == TILES - 1)
+        def _():
+            a_step(0, 5)
+            a_step(1, 5)
 
         return carry
 
@@ -331,8 +331,6 @@
     send_sums(1)
     take_sums(0)
     take_sums(1)
-    share_sums(0)
-    share_sums(1)
 
     book = i * SHARE + s
     lower = jnp.full((PIVOTS, 128), low[book], jnp.int32).astype(F32) * 0.125
@@ -341,6 +339,8 @@
     levels = lax.broadcasted_iota(jnp.int32, (PIVOTS, 128), 0).astype(F32)
     for h in range(2):
         drain(DV.at[h, pl.ds(0, N_SCEN - 1)], d_recv.at[h])
+    share_sums(0)
+    share_sums(1)
     for _ in range(ROUNDS):
         spacing = (upper - lower) / (PIVOTS - 1)
         marks = lower + levels * spacing

time: 72.2 us -> 70.7 us (0.979)
  Pallas kernels: 70.3 us -> 68.8 us
    pallas_call x1, Pallas kernels: 70.3 us -> 68.8 us  [body(): pl.pallas_call(kernel, out_shape=(pltpu.VMEM((SHARE, INST_DEV), F32), plt...]
where the time goes in v6:
time: 70.7 us; the launch traced here: 70.6 us
  Pallas kernels  68.8 us (97%)
  local copies, waits for them, and re-layouts  1.22 us (2%)
    pallas_call x1, Pallas kernels, body(): pl.pallas_call(kernel, out_shape=(pltpu.VMEM((SHARE, INST_DEV), F32), plt...  68.8 us

profile of v6, /device:TPU:8, one launch (start us, length us, event | category | flops | bytes accessed | tf_op | source)
XLA Modules:
  0.0 70.6 jit_solution(17658509430740179778)
XLA Ops:
  0.6 68.8 %revalue.1 = (f32[16,4096]{1,0:T(8,128)S(1)}, f32[16]{0:T(128)S(1)}) custom-call(bf16[512,128]{1,0:T(8,128)(2,1)} %shocks.1, bf16[2048,4096]{1,0:T(8,128)(2,1)} %loadings.1, f32[1,4096]{1,0:T(1,128)} %bitcast.4, f32[1,4096]{1,0:T(1,128)} %bitcast.5, f32[1,4096]{1,0:T(1,128)} %bitcast.6, s32[1,4096]{1,0:T(1,128)} %bitcast.7, s32[256]{0:T(256)} %low_in.1, ...), custom_call_target="tpu_custom_call" | custom-call | tf_op jit(solution)/shard_map/revalue/pallas_call | solution.py:501
  69.4 0.7 copy.13
  70.1 0.5 copy.14
